TPU v7x, 256 devices: a whole 4x4x8 slice. The times are simulated.
256 devices in a mesh: dp: 4 (over x), seq: 64 (over z, y, core).
Axes of the slice: x: 4, y: 4, z: 8, core: 2. Of those that a mesh axis runs over, the one named last changes fastest.
Arguments:
- streams: bfloat16 [3, 4, 8192, 4096], P(None, 'dp', 'seq'), may hold values from -6 to 6
- short_filter: float32 [3, 3, 4096], P(None, None, 'dp'), may hold values from -3.5 to 3.5
- decay_rate: float32 [2, 4096], P(None, 'dp'), may hold values from 1.2207031e-06 to 0.05
- pole_angle: float32 [2, 4096], P(None, 'dp'), may hold values from -3.140625 to 3.140625
- residue_re: float32 [2, 4096], P(None, 'dp'), may hold values from -6 to 6
- residue_im: float32 [2, 4096], P(None, 'dp'), may hold values from -6 to 6
- skip_gain: float32 [4096], P('dp'), may hold values from -6 to 6
- doc_starts: int32 [4, 8], P('dp'), may hold values from 0 to 8191, as said below
Outputs:
- mixed: bfloat16 [4, 8192, 4096], P('dp', 'seq')
Inputs may be any that keep to these rules, and one draw needn't show every extreme that they name: `doc_starts`: each row starts with 0 and rises strictly; the last document of every sequence is one position long.
All inputs are finite; a program needn't handle non-finite values.
Results may differ from a plain program's by a relative error of at most 0.0045.
Values may be sent and summed in bfloat16 or wider, within the bound.
A program may use at most 128 MiB of HBM per device.

v0:
```python
import jax
import jax.numpy as jnp
from jax import lax
from jax.sharding import PartitionSpec as P

block_len = 32


def from_behind(x, axis, by):
    count = lax.axis_size(axis)
    pairs = [(i, i + by) for i in range(count) if 0 <= i + by < count]
    return lax.ppermute(x, axis, pairs)


def prefix_2(part, axis, combine, identity):
    place = lax.axis_index(axis)
    gathered = jax.tree.map(lambda a: lax.all_gather(a, axis), part)
    state = jax.tree.map(lambda a, e: jnp.zeros_like(a) + jnp.asarray(e, a.dtype), part, identity)

    def one(turn, state):
        return combine(
            state, jax.tree.map(lambda a: lax.dynamic_index_in_dim(a, turn, 0, False), gathered)
        )

    return lax.fori_loop(0, place, one, state)


def pole_power(decay, rotation, powers):
    magnitude = jnp.exp(-decay * powers)
    return (magnitude * jnp.cos(rotation * powers), magnitude * jnp.sin(rotation * powers))


def segment_of(positions, starts):
    return jnp.sum((positions[..., None] >= starts).astype(jnp.int32), axis=-1) - 1


def local(
    streams, short_filter, decay_rate, pole_angle, residue_re, residue_im, skip_gain, doc_starts
):
    short_filter, decay_rate, pole_angle, residue_re, residue_im, skip_gain = (
        lax.all_gather(short_filter, "dp", axis=2, tiled=True),
        lax.all_gather(decay_rate, "dp", axis=1, tiled=True),
        lax.all_gather(pole_angle, "dp", axis=1, tiled=True),
        lax.all_gather(residue_re, "dp", axis=1, tiled=True),
        lax.all_gather(residue_im, "dp", axis=1, tiled=True),
        lax.all_gather(skip_gain, "dp", axis=0, tiled=True),
    )
    tok_rows = streams.shape[2]
    channels = streams.shape[3]
    modes = decay_rate.shape[0]
    my_index = lax.axis_index("seq")
    offset = my_index * tok_rows
    starts = doc_starts[0]
    rim_rows = streams[:, :, tok_rows - 2 :, :]
    before = from_behind(rim_rows, "seq", 1)
    extended = jnp.concatenate([before, streams], axis=2)[:, 0]
    filtered = (
        short_filter[0][:, None, :] * extended[:, 2:]
        + short_filter[1][:, None, :] * extended[:, 1:-1]
        + short_filter[2][:, None, :] * extended[:, :-2]
    )
    product = filtered[0] * filtered[1]
    out_gate = filtered[2]
    positions = offset + jnp.arange(tok_rows, dtype=jnp.int32)
    seg_ids = segment_of(positions, starts)
    seg_before = segment_of(offset - 1 + jnp.zeros((1,), jnp.int32), starts)[0]
    nblocks = tok_rows // block_len
    local_steps = jnp.arange(block_len, dtype=jnp.float32)[:, None, None]
    fwd_re, fwd_im = pole_power(decay_rate, pole_angle, local_steps)
    back_re, back_im = pole_power(-decay_rate, -pole_angle, local_steps)
    blocked = product.reshape(nblocks, block_len, 1, channels)
    lifted = jnp.concatenate([blocked * back_re, blocked * back_im], axis=2)
    lifted = lifted.reshape(nblocks, block_len, 2 * modes * channels)
    seg_blocks = seg_ids.reshape(nblocks, block_len)
    causal = jnp.arange(block_len)[:, None] >= jnp.arange(block_len)[None, :]
    within = (causal[None] & (seg_blocks[:, :, None] == seg_blocks[:, None, :])).astype(jnp.float32)
    summed = jnp.einsum("bts,bsk->btk", within, lifted, precision=lax.Precision.HIGHEST)
    summed = summed.reshape(nblocks, block_len, 2 * modes, channels)
    sum_re = summed[:, :, :modes]
    sum_im = summed[:, :, modes:]
    state_re = fwd_re * sum_re - fwd_im * sum_im
    state_im = fwd_re * sum_im + fwd_im * sum_re
    step_re, step_im = pole_power(decay_rate, pole_angle, jnp.float32(block_len))
    entry_seg = jnp.concatenate([seg_before[None], seg_blocks[:-1, -1]])
    keeps_last = (seg_blocks[:, -1] == entry_seg).astype(jnp.float32)

    def advance(running, inputs):
        run_re, run_im = running
        last_re, last_im, kept_now = inputs
        next_re = last_re + kept_now * (step_re * run_re - step_im * run_im)
        next_im = last_im + kept_now * (step_re * run_im + step_im * run_re)
        return ((next_re, next_im), (run_re, run_im))

    zero_state = jnp.zeros((modes, channels), jnp.float32)
    (end_re, end_im), (entry_re, entry_im) = lax.scan(
        advance, (zero_state, zero_state), (state_re[:, -1], state_im[:, -1], keeps_last)
    )
    lead_re, lead_im = pole_power(decay_rate, pole_angle, local_steps + 1.0)
    joined = (seg_blocks == entry_seg[:, None]).astype(jnp.float32)[:, :, None, None]
    state_re = state_re + joined * (lead_re * entry_re[:, None] - lead_im * entry_im[:, None])
    state_im = state_im + joined * (lead_re * entry_im[:, None] + lead_im * entry_re[:, None])
    whole_re, whole_im = pole_power(decay_rate, pole_angle, jnp.float32(tok_rows))
    keep_all = (seg_ids[-1] == seg_before).astype(jnp.float32)

    def combine(earlier, latter):
        early_are, early_aim, early_sre, early_sim = earlier
        late_are, late_aim, late_sre, late_sim = latter
        return (
            late_are * early_are - late_aim * early_aim,
            late_are * early_aim + late_aim * early_are,
            late_sre + late_are * early_sre - late_aim * early_sim,
            late_sim + late_are * early_sim + late_aim * early_sre,
        )

    unit_state = jnp.ones_like(end_re)
    prefix = prefix_2(
        (keep_all * whole_re, keep_all * whole_im, end_re, end_im),
        "seq",
        combine,
        (unit_state, zero_state, zero_state, zero_state),
    )
    inflow_re = prefix[2]
    inflow_im = prefix[3]
    all_steps = (
        jnp.arange(tok_rows, dtype=jnp.float32).reshape(nblocks, block_len)[:, :, None, None] + 1.0
    )
    enter_re, enter_im = pole_power(decay_rate, pole_angle, all_steps)
    reach = (seg_blocks == seg_before).astype(jnp.float32)[:, :, None, None]
    state_re = state_re + reach * (enter_re * inflow_re - enter_im * inflow_im)
    state_im = state_im + reach * (enter_re * inflow_im + enter_im * inflow_re)
    norm_factor = jnp.sqrt(-jnp.expm1(-2.0 * decay_rate))
    long_part = jnp.sum(norm_factor * (residue_re * state_re - residue_im * state_im), axis=2)
    long_part = long_part.reshape(tok_rows, channels)
    response = skip_gain * product + long_part
    return (out_gate * response).astype(jnp.bfloat16)[None]


def solution(mesh):
    placed = (
        P(None, "dp", "seq", None),
        P(None, None, "dp"),
        P(None, "dp"),
        P(None, "dp"),
        P(None, "dp"),
        P(None, "dp"),
        P("dp"),
        P("dp", None),
    )
    return jax.shard_map(
        local, mesh=mesh, in_specs=placed, out_specs=P("dp", "seq", None), check_vma=False
    )
```

profile of v0, /device:TPU:249, one launch (start us, length us, event | category | flops | bytes accessed | tf_op | source)
XLA Modules:
  0.0 430.3 jit_solution(6064338715635104115)
XLA Ops:
  6.5 1.3 fusion.14
  10.5 9.6 %all_gather.46 = f32[2,4096]{1,0:T(2,128)S(1)} all-gather(f32[2,1024]{1,0:T(2,128)} %param.15), channel_id=1, replica_groups=mesh['dp'=4,'seq'=64] {'dp'}, dimensions={1}, use_global_device_ids=true | all-gather | bytes 40960 | tf_op jit(solution)/shard_map/all_gather | solution.py:43
  20.1 9.2 %all_gather.44 = f32[2,4096]{1,0:T(2,128)S(1)} all-gather(f32[2,1024]{1,0:T(2,128)} %param.14), channel_id=1, replica_groups=mesh['dp'=4,'seq'=64] {'dp'}, dimensions={1}, use_global_device_ids=true | all-gather | bytes 40960 | tf_op jit(solution)/shard_map/all_gather | solution.py:42
  29.3 1.7 multiply_bitcast_fusion
  31.0 1.0 slice.69
  32.0 1.3 collective-permute-start
  33.8 16.3 %cosine_multiply_fusion = (f32[32,2,4096]{2,1,0:T(2,128)}, f32[32,2,4096]{2,1,0:T(2,128)}) fusion(f32[2,4096]{1,0:T(2,128)S(1)} %get-tuple-element.233, f32[2,4096]{1,0:T(2,128)S(1)} %all_gather.44), kind=kLoop, calls=%fused_computation.37 | loop fusion | flops 1048576 | bytes 2162688 | tf_op jit(solution)/shard_map/mul | solution.py:30
  50.2 9.8 %all_gather.42 = f32[3,3,4096]{2,1,0:T(4,128)S(1)} all-gather(f32[3,3,1024]{2,1,0:T(4,128)} %param.13), channel_id=1, replica_groups=mesh['dp'=4,'seq'=64] {'dp'}, dimensions={2}, use_global_device_ids=true | all-gather | bytes 184320 | tf_op jit(solution)/shard_map/all_gather | solution.py:41
  60.0 8.6 %fusion.6 = (f32[32,2,4096]{2,0,1:T(8,128)S(1)}, f32[32,2,4096]{2,0,1:T(8,128)S(1)}, f32[32,2,4096]{2,0,1:T(8,128)}, f32[32,2,4096]{2,0,1:T(8,128)}) fusion(f32[32]{0:T(128)S(1)} %iota_add_fusion, f32[2,4096]{1,0:T(2,128)S(1)} %all_gather.46, f32[2,4096]{1,0:T(2,128)S(1)} %get-tuple-element.234), kind=kLoop, calls=%fused_computation.32 | loop fusion | flops 2097152 | bytes 4259968 | tf_op jit(solution)/shard_map/mul | solution.py:30
  68.7 2.7 maximum_bitcast_fusion
  71.4 2.1 multiply_add_fusion
  73.8 1.7 copy-done.4
  75.6 1.1 copy-done.5
  76.7 3.9 broadcast_multiply_fusion.1
  80.5 9.7 %pad_maximum_fusion = f32[4,32,4,4096]{3,2,1,0:T(4,128)} fusion(f32[4,32,2,4096]{3,2,1,0:T(2,128)} %get-tuple-element.218, f32[4,32,2,4096]{3,2,1,0:T(2,128)S(1)} %get-tuple-element.217), kind=kLoop, calls=%fused_computation.14 | loop fusion | flops 2097152 | bytes 16777216 | tf_op jit(solution)/shard_map/concatenate | solution.py:72
  90.3 11.0 %reshape.158 = f32[4,32,16384]{2,1,0:T(8,128)} reshape(f32[4,32,4,4096]{3,2,1,0:T(4,128)} %pad_maximum_fusion) | data formatting | bytes 16777216 | tf_op jit(solution)/shard_map/reshape | solution.py:73
  101.3 10.8 %fusion.8 = f32[4,32,16384]{2,1,0:T(8,128)} fusion(f32[4,32,16384]{2,1,0:T(8,128)} %reshape.158, s32[4,32]{1,0:T(4,128)S(1)} %sub.35, pred[32,32]{1,0:T(8,128)(4,1)S(1)} %iota_compare_fusion), kind=kOutput, calls=%fused_computation.48 | convolution fusion | flops 805314560 | bytes 16778752 | tf_op jit(solution)/shard_map/bts,bsk->btk/dot_general | solution.py:77
  112.1 10.8 %reshape.159 = f32[4,32,4,4096]{3,2,1,0:T(4,128)} reshape(f32[4,32,16384]{2,1,0:T(8,128)} %fusion.8) | data formatting | bytes 16777216 | tf_op jit(solution)/shard_map/reshape | solution.py:78
  122.9 11.1 %fusion.15 = (f32[4,32,2,4096]{3,2,1,0:T(2,128)S(1)}, f32[4,32,2,4096]{3,2,1,0:T(2,128)}) fusion(f32[4,32,4,4096]{3,2,1,0:T(4,128)} %reshape.159), kind=kLoop, calls=%fused_computation.75 | loop fusion | bytes 16777216 | tf_op jit(solution)/shard_map/slice | solution.py:79
  134.0 7.8 %multiply_subtract_fusion = (f32[4,32,2,4096]{3,1,2,0:T(8,128)S(1)}, f32[4,32,2,4096]{3,1,2,0:T(8,128)S(1)}) fusion(f32[4,32,2,4096]{3,2,1,0:T(2,128)} %get-tuple-element.216, f32[4,32,2,4096]{3,2,1,0:T(2,128)S(1)} %get-tuple-element.215, f32[32,2,4096]{2,0,1:T(8,128)S(1)} %copy-done.3, f32[32,2,4096]{2,0,1:T(8,128)} %get-tuple-element.225), kind=kLoop, calls=%fused_computation.22 | loop fusion | flops 6291456 | bytes 18874368 | tf_op jit(solution)/shard_map/sub | solution.py:81
  141.9 2.0 copy-done.1
  144.0 1.1 copy-done.2
  145.5 7.9 %while.33 = (s32[]{:T(128)}, f32[2,4096]{1,0:T(2,128)S(1)}, f32[2,4096]{1,0:T(2,128)S(1)}, f32[4,2,4096]{2,1,0:T(2,128)S(1)}, f32[4,2,4096]{2,1,0:T(2,128)}, /*i...) while((s32[]{:T(128)}, f32[2,4096]{1,0:T(2,128)S(1)}, ...), condition=%wide.region_3.4_spmd.clone, body=%wide.region_2.3_spmd.clone.sunk | while | flops 114691 | bytes 393876 | solution.py:95
  154.6 9.0 %all_gather.43 = f32[4096]{0:T(1024)S(1)} all-gather(f32[1024]{0:T(1024)S(1)} %copy-done.10), channel_id=1, replica_groups=mesh['dp'=4,'seq'=64] {'dp'}, dimensions={0}, use_global_device_ids=true | all-gather | bytes 20480 | tf_op jit(solution)/shard_map/all_gather | solution.py:46
  163.7 9.6 %all_gather.45 = f32[2,4096]{1,0:T(2,128)S(1)} all-gather(f32[2,1024]{1,0:T(2,128)S(1)} %copy-done.8), channel_id=1, replica_groups=mesh['dp'=4,'seq'=64] {'dp'}, dimensions={1}, use_global_device_ids=true | all-gather | bytes 40960 | tf_op jit(solution)/shard_map/all_gather | solution.py:44
  173.2 9.0 %all_gather.55 = f32[2,4096]{1,0:T(2,128)S(1)} all-gather(f32[2,1024]{1,0:T(2,128)S(1)} %copy-done.9), channel_id=1, replica_groups=mesh['dp'=4,'seq'=64] {'dp'}, dimensions={1}, use_global_device_ids=true | all-gather | bytes 40960 | tf_op jit(solution)/shard_map/all_gather | solution.py:45
  182.4 6.7 %all-gather.17.cloned.1.call-done = f32[64,2,4096]{2,1,0:T(2,128)} async-done(((f32[1,2,4096]{2,1,0:T(2,128)}), f32[64,2,4096]{2,1,0:T(2,128)}) %all-gather.17.cloned.1.call-update) | async-done | bytes 2097168 | tf_op jit(solution)/shard_map/all_gather | solution.py:17
  189.1 77.8 %all-gather.13.cloned.1.call-done = f32[64,2,4096]{2,1,0:T(2,128)} async-done(((f32[1,2,4096]{2,1,0:T(2,128)}), f32[64,2,4096]{2,1,0:T(2,128)}) %all-gather.13.cloned.1.call-update) | async-done | bytes 2097168 | tf_op jit(solution)/shard_map/all_gather | solution.py:17
  266.9 77.6 %all-gather.19.cloned.1.call-done = f32[64,2,4096]{2,1,0:T(2,128)} async-done(((f32[1,2,4096]{2,1,0:T(2,128)}), f32[64,2,4096]{2,1,0:T(2,128)}) %all-gather.19.cloned.1.call-update) | async-done | bytes 2097168 | tf_op jit(solution)/shard_map/all_gather | solution.py:17
  344.5 56.3 %while.32 = (s32[]{:T(128)}, f32[2,4096]{1,0:T(2,128)S(1)}, f32[2,4096]{1,0:T(2,128)S(1)}, s32[]{:T(128)}, f32[64,2,4096]{2,1,0:T(2,128)}, /*index=5*/f32[64,2,4...) while((s32[]{:T(128)}, f32[2,4096]{1,0:T(2,128)S(1)}, ...), condition=%wide.region_5.6_spmd, body=%wide.region_4.5_spmd.sunk | while | flops 65541 | bytes 262291 | solution.py:25
  344.5 0.9 fusion.18
  345.4 0.9 fusion.18
  346.3 0.9 fusion.18
  347.2 0.9 fusion.18
  348.1 0.9 fusion.18
  349.0 0.9 fusion.18
  349.9 0.9 fusion.18
  350.8 0.9 fusion.18
  351.7 0.9 fusion.18
  352.6 0.9 fusion.18
  353.5 0.9 fusion.18
  355.3 0.9 fusion.18
  358.8 0.9 fusion.18
  359.8 0.9 fusion.18
  362.4 0.9 fusion.18
  363.3 0.9 fusion.18
  366.0 0.9 fusion.18
  366.9 0.9 fusion.18
  369.6 0.9 fusion.18
  372.2 0.9 fusion.18
  373.1 0.9 fusion.18
  374.0 0.9 fusion.18
  376.7 0.9 fusion.18
  377.6 0.9 fusion.18
  380.3 0.9 fusion.18
  383.8 0.9 fusion.18
  387.4 0.9 fusion.18
  390.1 0.9 fusion.18
  391.0 0.9 fusion.18
  393.7 0.9 fusion.18
  394.6 0.9 fusion.18
  397.2 0.9 fusion.18
  400.8 21.4 %multiply_reduce_fusion = f32[4,32,4096]{2,1,0:T(8,128)S(1)} fusion(f32[4,32,2,4096]{3,1,2,0:T(8,128)} %copy-done.2, f32[4,32,2,4096]{3,1,2,0:T(8,128)} %copy-done.1, f32[2,4096]{1,0:T(2,128)S(1)} %all_gather.55, f32[2,4096]{1,0:T(2,128)S(1)} %get-tuple-element.135, f32[2,4096]{1,0:T(2,128)S(1)} %get-tuple-element.134, f32[2,4096]{1,0:T(2,128)S(1)} %all_gather.46, ...), kind=kLoop, calls=%fused_computation.20 | loop fusion | flops 29884416 | bytes 13075968 | tf_op jit(solution)/shard_map/reduce_sum | solution.py:132
  422.2 1.6 fusion.5
  (99 shorter events, 38.9 us)
Async XLA Ops:
  6.5 175.8 %all-gather.15.cloned.1.call-start = ((), (), s32[]{:S(2)}) async-start(), calls=%async_computation.1 | async-start | bytes 2129920 | tf_op jit(solution)/shard_map/all_gather | solution.py:17
  31.0 158.1 %all-gather.17.cloned.1.call-start = ((), (), s32[]{:S(2)}) async-start(), calls=%async_computation.2 | async-start | bytes 2129920 | tf_op jit(solution)/shard_map/all_gather | solution.py:17
  32.0 36.7 %collective-permute-start = (bf16[3,1,2,4096]{3,2,0,1:T(2,128)(2,1)S(1)}, bf16[3,1,2,4096]{3,2,0,1:T(2,128)(2,1)S(1)}, u32[]{:S(2)}, u32[]{:S(2)}) collective-permute-start(bf16[3,1,2,4096]{3,2,0,1:T(2,128)(2,1)S(1)} %slice.69), channel_id=1, source_target_pairs={{0,1},{1,2},{2,3},{3,4},{4,5},{5,6},{6,7},{7,8},{8,9},{9,10},{10,1... | collective-permute-start | bytes 147464 | tf_op jit(solution)/shard_map/ppermute | solution.py:12
  33.3 233.5 %all-gather.13.cloned.1.call-start = ((), (), s32[]{:S(2)}) async-start(), calls=%async_computation | async-start | bytes 2129920 | tf_op jit(solution)/shard_map/all_gather | solution.py:17
  73.5 7.0 %copy-start = (f32[3,128,4096]{2,1,0:T(8,128)}, f32[3,128,4096]{2,1,0:T(8,128)S(1)}, u32[]{:S(2)}) copy-start(f32[3,128,4096]{2,1,0:T(8,128)S(1)} %multiply_add_fusion) | copy-start | bytes 18874372
  73.6 2.0 copy-start.4
  73.6 3.1 copy-start.5
  122.9 11.1 %copy-start.3 = (f32[32,2,4096]{2,0,1:T(8,128)S(1)}, f32[32,2,4096]{2,0,1:T(8,128)}, u32[]{:S(2)}) copy-start(f32[32,2,4096]{2,0,1:T(8,128)} %get-tuple-element.224) | copy-start | bytes 3145732
  134.0 20.6 %copy-start.10 = (f32[1024]{0:T(1024)S(1)}, f32[1024]{0:T(1024)}, u32[]{:S(2)}) copy-start(f32[1024]{0:T(1024)} %param.18) | copy-start | bytes 12292
  134.0 29.7 %copy-start.8 = (f32[2,1024]{1,0:T(2,128)S(1)}, f32[2,1024]{1,0:T(2,128)}, u32[]{:S(2)}) copy-start(f32[2,1024]{1,0:T(2,128)} %param.16) | copy-start | bytes 24580
  134.0 39.2 %copy-start.9 = (f32[2,1024]{1,0:T(2,128)S(1)}, f32[2,1024]{1,0:T(2,128)}, u32[]{:S(2)}) copy-start(f32[2,1024]{1,0:T(2,128)} %param.17) | copy-start | bytes 24580
  141.8 2.0 copy-start.1
  141.8 3.3 copy-start.2
  153.4 0.6 copy-start.6
  153.4 0.7 copy-start.7
  154.0 190.4 %all-gather.19.cloned.1.call-start = ((), (), s32[]{:S(2)}) async-start(), calls=%async_computation.3 | async-start | bytes 2129920 | tf_op jit(solution)/shard_map/all_gather | solution.py:17
  400.8 21.4 %slice-start = ((s8[6291456]{0:T(1024)(128)(4,1)}), s8[4194304]{0:T(1024)(128)(4,1)S(1)}, s32[]{:S(2)}) async-start(s8[6291456]{0:T(1024)(128)(4,1)} %bitcast.73), calls=%async_computation.4 | async-start | bytes 8388608
  400.8 21.4 %slice-start.1 = ((s8[6291456]{0:T(1024)(128)(4,1)}), s8[2097152]{0:T(1024)(128)(4,1)S(1)}, s32[]{:S(2)}) async-start(s8[6291456]{0:T(1024)(128)(4,1)} %bitcast.73), calls=%async_computation.5 | async-start | bytes 4194304
Sparse Core Ops, SparseCore 0:
  31.1 80.2 all-gather.14
  114.1 74.9 all-gather.16
  191.9 74.9 all-gather.12
  269.5 74.9 all-gather.18
where the time goes:
time: 436 us; the launch traced here: 430 us
  waiting for transfers between devices  163 us (37%)
  other arithmetic  139 us (32%)
  blocking collectives  56.2 us (13%)
  local copies, waits for them, and re-layouts  44.3 us (10%)
  between operations  14.7 us (3%)
  matrix products  10.8 us (2%)
    all_gather x4, waiting for transfers between devices, prefix_2(): gathered = jax.tree.map(lambda a: lax.all_gather(a, axis), part)  162 us
    add x63, other arithmetic, combine(): late_sim + late_are * early_sim + late_aim * early_sre  54.8 us
    mul x2, other arithmetic, pole_power(): magnitude * jnp.cos(rotation * powers)  24.9 us
    reduce_sum x1, other arithmetic, local(): jnp.sum(norm_factor * (residue_re * state_re - residue_im * state_im), ax...  21.4 us
    slice x1, local copies, waits for them, and re-layouts, local(): sum_re = summed[:, :, :modes]  11.1 us
    reshape x1, local copies, waits for them, and re-layouts, local(): lifted = lifted.reshape(nblocks, block_len, 2 * modes * channels)  11 us
    dot_general x1, matrix products, local(): jnp.einsum('bts,bsk->btk', within, lifted, precision=lax.Precision.HIGHEST)  10.8 us
    reshape x1, local copies, waits for them, and re-layouts, local(): summed = summed.reshape(nblocks, block_len, 2 * modes, channels)  10.8 us
  transfers between devices with their start and end apart: 5, of which 3 were waited for; matrix products, arithmetic and copies ran while one was open for 24% of the time, Pallas kernels for 0%

commit v1 on v0

v1 whole, which is shorter than its diff:
```python
import functools

import jax
import jax.numpy as jnp
from jax import lax
from jax.experimental import pallas as pl
from jax.experimental.pallas import tpu as pltpu
from jax.sharding import PartitionSpec as P

MESH = pl.DeviceIdType.MESH
F32 = jnp.float32
BF16 = jnp.bfloat16
LANES = 128
CHUNKS = 8
STEPS = 16
TOK = CHUNKS * STEPS


def iota(shape, axis):
    return lax.broadcasted_iota(jnp.int32, shape, axis)


def rows(ref, row, count=8):
    return jnp.broadcast_to(ref[pl.ds(row, 1), :], (count, LANES))


def cmul(ar, ai, br, bi):
    return ar * br - ai * bi, ar * bi + ai * br


def kernel(
    n_dp,
    n_seq,
    plane,
    streams_hbm,
    taps_hbm,
    decay_hbm,
    angle_hbm,
    resr_hbm,
    resi_hbm,
    skip_hbm,
    starts_hbm,
    out_hbm,
    xbuf,
    hsend,
    hrecv,
    taps_v,
    decay_v,
    angle_v,
    resr_v,
    resi_v,
    skip_v,
    raw,
    starts_s,
    par_a,
    par_b,
    derived,
    perm_in,
    perm_out,
    m_keep,
    m_tail,
    m_first,
    m_scan,
    m_dev,
    vbuf,
    gr,
    gm,
    excl,
    table,
    state,
    r1,
    pre,
    total,
    r2,
    back,
    inflow,
    obuf,
    in_sem,
    x_sem,
    pa_send,
    pa_recv,
    pb_send,
    pb_recv,
    h_send,
    h_recv,
    s1_send,
    s1_recv,
    s2_send,
    s2_recv,
    s3_send,
    s3_recv,
    o_sem,
):
    n_z = n_seq // plane
    width = plane * LANES
    me_x = lax.axis_index("dp")
    me = lax.axis_index("seq")
    me_z = me // plane
    me_q = me % plane
    offsets = [0]
    for d in range(1, n_dp // 2 + 1):
        offsets.append(d)
        if n_dp - d != d:
            offsets.append(n_dp - d)

    x_peer = [None] + [((me_x + n_dp - o) % n_dp, me) for o in offsets[1:]]
    q_rank = [(me_q + k) % plane for k in range(1, plane)]
    q_peer = [(me_x, me_z * plane + r) for r in q_rank]
    z_peer = [(me_x, ((me_z + k) % n_z) * plane + me_q) for k in range(1, n_z)]
    after = (me_x, (me + 1) % n_seq)
    before = (me_x, (me + n_seq - 1) % n_seq)
    block = [(me_x + o) % n_dp for o in offsets]

    barrier = pltpu.get_barrier_semaphore()
    peers = x_peer[1:] + q_peer + z_peer + [after, before]
    for peer in peers:
        pl.semaphore_signal(barrier, inc=1, device_id=peer, device_id_type=MESH)

    loads = [
        pltpu.make_async_copy(a, b, in_sem.at[n])
        for n, (a, b) in enumerate(
            [
                (taps_hbm, taps_v),
                (decay_hbm, decay_v),
                (angle_hbm, angle_v),
                (resr_hbm, resr_v),
                (resi_hbm, resi_v),
                (skip_hbm, skip_v),
                (starts_hbm, starts_s),
            ]
        )
    ]
    for copy in loads:
        copy.start()
    x_loads = []
    for j in range(n_dp):
        columns = pl.ds(pl.multiple_of(block[j] * width, width), width)
        copy = pltpu.make_async_copy(streams_hbm.at[:, 0, :, columns], xbuf.at[j], x_sem.at[j])
        copy.start()
        x_loads.append(copy)

    lines = TOK + 16
    row = iota((lines, lines), 0)
    col = iota((lines, lines), 1)
    place = (row % CHUNKS) * STEPS + row // CHUNKS - 2
    has_before = jnp.where(me > 0, 1, 0)
    for s in range(3):
        pick = jnp.where(place >= 0, place, jnp.where(has_before > 0, TOK + 2 * s + 2 + place, -1))
        perm_in[s] = jnp.where(col == pick, 1.0, 0.0).astype(BF16)
    row = iota((TOK, TOK), 0)
    col = iota((TOK, TOK), 1)
    perm_out[...] = jnp.where(col == (row % STEPS) * CHUNKS + row // STEPS, 1.0, 0.0).astype(BF16)

    for copy in loads[:6]:
        copy.wait()
    for i in range(plane):
        lane = slice(i * LANES, (i + 1) * LANES)
        for s in range(2):
            for k in range(3):
                par_a[0, (3 * s + k) * plane + i, :] = taps_v[k, s, lane]
        for k in range(3):
            par_b[0, k * plane + i, :] = taps_v[k, 2, lane]
        par_b[0, 7 * plane + i, :] = skip_v[0, lane]
        for m in range(2):
            r = 2 * i + m
            for n, source in enumerate((decay_v, angle_v, resr_v, resi_v)):
                raw[n, r, :] = source[m, lane]
    decay = raw[0]
    magnitude = jnp.exp(-decay)
    par_a[0, 6 * plane : 8 * plane, :] = magnitude * jnp.cos(raw[1])
    par_a[0, 8 * plane : 10 * plane, :] = magnitude * jnp.sin(raw[1])
    square = decay * decay
    sinh = decay * (1.0 + square * (1.0 / 6.0) * (1.0 + square * (1.0 / 20.0) * (1.0 + square * (1.0 / 42.0))))
    norm = jnp.sqrt(2.0 * magnitude * sinh)
    par_b[0, 3 * plane : 5 * plane, :] = norm * raw[2]
    par_b[0, 5 * plane : 7 * plane, :] = norm * raw[3]

    row = iota((16, 16), 0)
    col = iota((16, 16), 1)
    for j in range(n_dp):
        x_loads[j].wait()
        for n in range(width // 256):
            lane = slice(n * 256, (n + 1) * 256)
            rim = jnp.zeros((16, 256), F32)
            for s in range(3):
                pick = jnp.where((row // 2 == s) & (col == 14 + row % 2), 1.0, 0.0).astype(BF16)
                rim += jnp.dot(pick, xbuf[j, s, TOK - 16 :, lane], preferred_element_type=F32)
            hsend[j, :, lane] = rim.astype(BF16)

    pl.semaphore_wait(barrier, len(peers))

    sends = []

    def send(source, target, send_sem, recv_sem, device):
        copy = pltpu.make_async_remote_copy(
            src_ref=source, dst_ref=target, send_sem=send_sem, recv_sem=recv_sem, device_id=device, device_id_type=MESH
        )
        copy.start()
        sends.append(copy)
        return copy

    a_copies = [None] + [
        send(par_a.at[0], par_a.at[j], pa_send.at[j], pa_recv.at[j], x_peer[j]) for j in range(1, n_dp)
    ]
    h_copies = [send(hsend.at[j], hrecv.at[j], h_send.at[j], h_recv.at[j], after) for j in range(n_dp)]
    b_copies = [None] + [
        send(par_b.at[0], par_b.at[j], pb_send.at[j], pb_recv.at[j], x_peer[j]) for j in range(1, n_dp)
    ]

    loads[6].wait()
    starts = [starts_s[0, d] for d in range(starts_s.shape[1])]
    near = [s - me * TOK for s in starts]
    chunk = iota((8, LANES), 0)
    one = jnp.ones((8, LANES), F32)
    zero = jnp.zeros((8, LANES), F32)

    def free(lo, hi, among):
        hit = (among[0] >= lo) & (among[0] < hi)
        for s in among[1:]:
            hit = hit | ((s >= lo) & (s < hi))
        return jnp.where(hit, zero, one)

    for k in range(STEPS):
        here = chunk * STEPS + k
        m_keep[k] = free(here, here + 1, near)
        m_tail[k] = free(here + 1, chunk * STEPS + STEPS, near)
        m_first[k] = free(jnp.zeros_like(here), here + 1, near)
    for n, shift in enumerate((1, 2, 4)):
        reach = free((chunk - shift + 1) * STEPS, (chunk + 1) * STEPS, near)
        m_scan[n] = jnp.where(chunk >= shift, reach, zero)
    first_of_plane = me_z * plane * TOK
    m_dev[0] = free(first_of_plane + chunk * TOK, first_of_plane + (chunk + 1) * TOK, starts)
    m_dev[1] = free(chunk * plane * TOK, (chunk + 1) * plane * TOK, starts)

    n_rows = 2 * plane
    log_plane = plane.bit_length() - 1

    def filters(j, s, i, source, base, x):
        c = [rows(source.at[j], (base + k) * plane + i) for k in range(3)]
        return [c[0] * x[k + 2] + c[1] * x[k + 1] + c[2] * x[k] for k in range(STEPS)]

    def permuted(j, s, i2):
        lane = pl.ds(pl.multiple_of(i2 * 256, 256), 256)
        operand = jnp.concatenate([xbuf[j, s, :, lane], hrecv[j, :, lane]], axis=0)
        return jnp.dot(perm_in[s], operand, preferred_element_type=F32)

    def half(x, h):
        return [x[8 * g : 8 * g + 8, h * LANES : (h + 1) * LANES] for g in range(STEPS + 2)]

    def states(j):
        pr = par_a[j, 6 * plane : 8 * plane, :]
        pi = par_a[j, 8 * plane : 10 * plane, :]
        qr, qi = pr, pi
        slot = 0
        for n in range(7 + log_plane):
            qr, qi = qr * qr - qi * qi, 2.0 * qr * qi
            if n + 1 in (4, 5, 6, 7, 7 + log_plane):
                derived[j, slot * n_rows : (slot + 1) * n_rows, :] = qr
                derived[j, (slot + 1) * n_rows : (slot + 2) * n_rows, :] = qi
                slot += 2
        derived[j, 10 * n_rows : 11 * n_rows, :] = 2.0 * pr
        derived[j, 11 * n_rows : 12 * n_rows, :] = pr * pr + pi * pi

        @pl.loop(0, width // 256)
        def _(i2):
            x0 = permuted(j, 0, i2)
            x1 = permuted(j, 1, i2)
            for h in range(2):
                i = 2 * i2 + h
                f0 = filters(j, 0, i, par_a, 0, half(x0, h))
                f1 = filters(j, 1, i, par_a, 3, half(x1, h))
                v = [a * b for a, b in zip(f0, f1)]
                for k in range(STEPS):
                    vbuf[j, i, 8 * k : 8 * k + 8, :] = v[k]
                masked = [v[k] * m_tail[k] for k in range(STEPS)]
                for m in range(2):
                    r = 2 * i + m
                    a1 = rows(derived.at[j], 10 * n_rows + r)
                    a2 = rows(derived.at[j], 11 * n_rows + r)
                    b1, b2 = masked[0], zero
                    for k in range(1, STEPS):
                        b1, b2 = a1 * b1 + (masked[k] - a2 * b2), b1
                    er = b1 - rows(par_a.at[j], 6 * plane + r) * b2
                    ei = rows(par_a.at[j], 8 * plane + r) * b2
                    for n, shift in enumerate((1, 2, 4)):
                        reach = m_scan[n]
                        kr = reach * rows(derived.at[j], 2 * n * n_rows + r)
                        ki = reach * rows(derived.at[j], (2 * n + 1) * n_rows + r)
                        sr = pltpu.roll(er, shift, axis=0)
                        si = pltpu.roll(ei, shift, axis=0)
                        ar, ai = cmul(kr, ki, sr, si)
                        er, ei = er + ar, ei + ai
                    state[j, i, pl.ds(m, 1), :] = er[7:8]
                    state[j, i, pl.ds(2 + m, 1), :] = ei[7:8]
                    later = jnp.where(chunk >= 1, one, zero)
                    excl[j, i, 16 * m : 16 * m + 8, :] = pltpu.roll(er, 1, axis=0) * later
                    excl[j, i, 16 * m + 8 : 16 * m + 16, :] = pltpu.roll(ei, 1, axis=0) * later

    def gather_plane(j):
        r1[j, me_q] = state[j, me_q]
        return [
            send(state.at[j, q_rank[n]], r1.at[j, me_q], s1_send.at[j, n], s1_recv.at[j, n], q_peer[n])
            for n in range(plane - 1)
        ]

    def combine_plane(j, copies):
        for copy in copies:
            copy.wait_recv()
        pr = derived[j, pl.ds(6 * n_rows + 2 * me_q, 2), :]
        pi = derived[j, pl.ds(7 * n_rows + 2 * me_q, 2), :]
        run_r = jnp.zeros((2, LANES), F32)
        run_i = run_r
        for e in range(plane):
            pre[j, e, 0:2, :] = run_r
            pre[j, e, 2:4, :] = run_i
            keep = m_dev[0, e : e + 1, :]
            ar, ai = cmul(pr * keep, pi * keep, run_r, run_i)
            run_r = ar + r1[j, e, 0:2, :]
            run_i = ai + r1[j, e, 2:4, :]
        total[j, 0:2, :] = run_r
        total[j, 2:4, :] = run_i
        r2[j, me_z] = total[j]
        return [
            send(total.at[j], r2.at[j, me_z], s2_send.at[j, n], s2_recv.at[j, n], z_peer[n]) for n in range(n_z - 1)
        ]

    def combine_all(j, copies):
        for copy in copies:
            copy.wait_recv()
        pr = derived[j, pl.ds(8 * n_rows + 2 * me_q, 2), :]
        pi = derived[j, pl.ds(9 * n_rows + 2 * me_q, 2), :]
        run_r = jnp.zeros((2, LANES), F32)
        run_i = run_r
        for z in range(n_z - 1):
            keep = m_dev[1, z : z + 1, :]
            ar, ai = cmul(pr * keep, pi * keep, run_r, run_i)
            past = z < me_z
            run_r = jnp.where(past, ar + r2[j, z, 0:2, :], run_r)
            run_i = jnp.where(past, ai + r2[j, z, 2:4, :], run_i)
        pr = derived[j, pl.ds(6 * n_rows + 2 * me_q, 2), :]
        pi = derived[j, pl.ds(7 * n_rows + 2 * me_q, 2), :]
        for e in range(plane):
            back[j, e, 0:2, :] = pre[j, e, 0:2, :] + run_r
            back[j, e, 2:4, :] = pre[j, e, 2:4, :] + run_i
            keep = m_dev[0, e : e + 1, :]
            run_r, run_i = cmul(pr * keep, pi * keep, run_r, run_i)
        inflow[j, me_q] = back[j, me_q]
        return [
            send(back.at[j, q_rank[n]], inflow.at[j, me_q], s3_send.at[j, n], s3_recv.at[j, n], q_peer[n])
            for n in range(plane - 1)
        ]

    def response(j):
        @pl.loop(0, width // 256)
        def _(i2):
            x2 = permuted(j, 2, i2)
            for h in range(2):
                i = 2 * i2 + h
                gate = filters(j, 2, i, par_b, 0, half(x2, h))
                skip = rows(par_b.at[j], 7 * plane + i)
                v = [vbuf[j, i, 8 * k : 8 * k + 8, :] for k in range(STEPS)]
                y = [skip * v[k] for k in range(STEPS)]
                for m in range(2):
                    r = 2 * i + m
                    pr = rows(par_a.at[j], 6 * plane + r)
                    pi = rows(par_a.at[j], 8 * plane + r)
                    wr = rows(par_b.at[j], 3 * plane + r)
                    wi = rows(par_b.at[j], 5 * plane + r)
                    sr = excl[j, i, 16 * m : 16 * m + 8, :]
                    si = excl[j, i, 16 * m + 8 : 16 * m + 16, :]
                    for k in range(STEPS):
                        keep = m_keep[k]
                        tr, ti = keep * sr, keep * si
                        sr = pr * tr - pi * ti + v[k]
                        si = pr * ti + pi * tr
                        y[k] = y[k] + (wr * sr - wi * si)
                    for n, bit in enumerate((1, 2, 4)):
                        on = (chunk & bit) > 0
                        br = jnp.where(on, rows(derived.at[j], 2 * n * n_rows + r), one)
                        bi = jnp.where(on, rows(derived.at[j], (2 * n + 1) * n_rows + r), zero)
                        wr, wi = cmul(wr, wi, br, bi)
                    table[j, i, 32 * m : 32 * m + 8, :] = wr
                    table[j, i, 32 * m + 8 : 32 * m + 16, :] = wi
                    wr, wi = cmul(wr, wi, pr, pi)
                    table[j, i, 32 * m + 16 : 32 * m + 24, :] = wr
                    table[j, i, 32 * m + 24 : 32 * m + 32, :] = wi
                for k in range(STEPS):
                    gr[j, i, 8 * k : 8 * k + 8, :] = gate[k] * y[k]
                    gm[j, i, 8 * k : 8 * k + 8, :] = gate[k] * m_first[k]

    def finish(j, copies):
        for copy in copies:
            copy.wait_recv()

        @pl.loop(0, width // 256)
        def _(i2):
            halves = []
            for h in range(2):
                i = 2 * i2 + h
                added = None
                for m in range(2):
                    r = 2 * i + m
                    ir = rows(inflow.at[j, i], m)
                    ii = rows(inflow.at[j, i], 2 + m)
                    a1 = rows(derived.at[j], 10 * n_rows + r)
                    a2 = rows(derived.at[j], 11 * n_rows + r)
                    t = [table[j, i, 32 * m + 8 * n : 32 * m + 8 * n + 8, :] for n in range(4)]
                    older = t[0] * ir - t[1] * ii
                    u = [t[2] * ir - t[3] * ii]
                    for k in range(1, STEPS):
                        u.append(a1 * u[-1] - a2 * older)
                        older = u[-2]
                    added = u if added is None else [a + b for a, b in zip(added, u)]
                halves.append(
                    jnp.concatenate(
                        [
                            gr[j, i, 8 * k : 8 * k + 8, :] + gm[j, i, 8 * k : 8 * k + 8, :] * added[k]
                            for k in range(STEPS)
                        ],
                        axis=0,
                    )
                )
            mixed = jnp.concatenate(halves, axis=1).astype(BF16)
            lane = pl.ds(pl.multiple_of(i2 * 256, 256), 256)
            obuf[j, :, lane] = jnp.dot(perm_out[...], mixed, preferred_element_type=F32).astype(BF16)

        columns = pl.ds(pl.multiple_of(block[j] * width, width), width)
        copy = pltpu.make_async_copy(obuf.at[j], out_hbm.at[0, :, columns], o_sem.at[j])
        copy.start()
        return copy

    one_copies = []
    for j in range(n_dp):
        if j:
            a_copies[j].wait_recv()
        h_copies[j].wait_recv()
        states(j)
        one_copies.append(gather_plane(j))
    two_copies = []
    for j in range(n_dp):
        two_copies.append(combine_plane(j, one_copies[j]))
        if j:
            b_copies[j].wait_recv()
        if j < n_dp - 1:
            response(j)
    response(n_dp - 1)
    three_copies = [combine_all(j, two_copies[j]) for j in range(n_dp)]
    stores = [finish(j, three_copies[j]) for j in range(n_dp)]
    for copy in sends:
        copy.wait_send()
    for copy in stores:
        copy.wait()


def local(n_dp, n_seq, streams, short_filter, decay_rate, pole_angle, residue_re, residue_im, skip_gain, doc_starts):
    width = short_filter.shape[2]
    plane = width // LANES
    n_z = n_seq // plane
    n_rows = 2 * plane
    vmem = pltpu.VMEM
    dma = pltpu.SemaphoreType.DMA
    anywhere = pl.BlockSpec(memory_space=pl.ANY)
    lines = TOK + 16
    return pl.pallas_call(
        functools.partial(kernel, n_dp, n_seq, plane),
        out_shape=jax.ShapeDtypeStruct((1, TOK, streams.shape[3]), BF16),
        in_specs=[anywhere] * 8,
        out_specs=anywhere,
        scratch_shapes=[
            vmem((n_dp, 3, TOK, width), BF16),
            vmem((n_dp, 16, width), BF16),
            vmem((n_dp, 16, width), BF16),
            vmem((3, 3, width), F32),
            vmem((2, width), F32),
            vmem((2, width), F32),
            vmem((2, width), F32),
            vmem((2, width), F32),
            vmem((1, width), F32),
            vmem((4, n_rows, LANES), F32),
            pltpu.SMEM(doc_starts.shape, jnp.int32),
            vmem((n_dp, 10 * plane, LANES), F32),
            vmem((n_dp, 8 * plane, LANES), F32),
            vmem((n_dp, 12 * n_rows, LANES), F32),
            vmem((3, lines, lines), BF16),
            vmem((TOK, TOK), BF16),
            vmem((STEPS, 8, LANES), F32),
            vmem((STEPS, 8, LANES), F32),
            vmem((STEPS, 8, LANES), F32),
            vmem((3, 8, LANES), F32),
            vmem((2, 8, LANES), F32),
            vmem((n_dp, plane, TOK, LANES), F32),
            vmem((n_dp, plane, TOK, LANES), F32),
            vmem((n_dp, plane, TOK, LANES), F32),
            vmem((n_dp, plane, 32, LANES), F32),
            vmem((n_dp, plane, 64, LANES), F32),
            vmem((n_dp, plane, 4, LANES), F32),
            vmem((n_dp, plane, 4, LANES), F32),
            vmem((n_dp, plane, 4, LANES), F32),
            vmem((n_dp, 4, LANES), F32),
            vmem((n_dp, n_z, 4, LANES), F32),
            vmem((n_dp, plane, 4, LANES), F32),
            vmem((n_dp, plane, 4, LANES), F32),
            vmem((n_dp, TOK, width), BF16),
            dma((7,)),
            dma((n_dp,)),
            dma((n_dp,)),
            dma((n_dp,)),
            dma((n_dp,)),
            dma((n_dp,)),
            dma((n_dp,)),
            dma((n_dp,)),
            dma((n_dp, plane - 1)),
            dma((n_dp, plane - 1)),
            dma((n_dp, n_z - 1)),
            dma((n_dp, n_z - 1)),
            dma((n_dp, plane - 1)),
            dma((n_dp, plane - 1)),
            dma((n_dp,)),
        ],
        compiler_params=pltpu.CompilerParams(collective_id=0, has_side_effects=True, vmem_limit_bytes=48 * 2**20),
        name="hyena_modal_scan",
    )(
        streams,
        short_filter,
        decay_rate,
        pole_angle,
        residue_re,
        residue_im,
        skip_gain.reshape(1, width),
        doc_starts,
    )


def solution(mesh):
    placed = (
        P(None, "dp", "seq", None),
        P(None, None, "dp"),
        P(None, "dp"),
        P(None, "dp"),
        P(None, "dp"),
        P(None, "dp"),
        P("dp"),
        P("dp", None),
    )
    return jax.shard_map(
        functools.partial(local, mesh.shape["dp"], mesh.shape["seq"]),
        mesh=mesh,
        in_specs=placed,
        out_specs=P("dp", "seq", None),
        check_vma=False,
    )
```

time: 436 us -> 40.1 us (0.09)
  the two profiles are of different devices: /device:TPU:249 before, /device:TPU:1 now
where the time goes in v1:
time: 40.1 us; the launch traced here: 39.7 us
  Pallas kernels  31.9 us (80%)
  local copies, waits for them, and re-layouts  7.79 us (19%)
    pallas_call x1, Pallas kernels, local(): pl.pallas_call(functools.partial(kernel, n_dp, n_seq, plane), out_shape=j...  31.9 us
    unnamed x17, local copies, waits for them, and re-layouts  7.79 us

profile of v1, /device:TPU:1, one launch (start us, length us, event | category | flops | bytes accessed | tf_op | source)
XLA Modules:
  0.0 39.7 jit_solution(10693384039203225683)
XLA Ops:
  0.0 0.0 copy-start
  0.0 1.9 %copy-done = bf16[3,1,128,4096]{3,2,1,0:T(8,128)(2,1)S(1)} copy-done((bf16[3,1,128,4096]{3,2,1,0:T(8,128)(2,1)S(1)}, bf16[3,1,128,4096]{3,2,1,0:T(8,128)(2,1)}, u32[]{:S(2)}) %copy-start) | copy-done | bytes 3145752
  1.9 0.0 copy-start.1
  1.9 0.8 %copy-done.1 = f32[3,3,1024]{2,1,0:T(4,128)S(1)} copy-done((f32[3,3,1024]{2,1,0:T(4,128)S(1)}, f32[3,3,1024]{2,1,0:T(4,128)}, u32[]{:S(2)}) %copy-start.1) | copy-done | bytes 36888
  2.7 0.0 copy-start.2
  2.7 0.7 %copy-done.2 = f32[2,1024]{1,0:T(2,128)S(1)} copy-done((f32[2,1024]{1,0:T(2,128)S(1)}, f32[2,1024]{1,0:T(2,128)}, u32[]{:S(2)}) %copy-start.2) | copy-done | bytes 8216
  3.4 0.0 copy-start.3
  3.4 0.7 %copy-done.3 = f32[2,1024]{1,0:T(2,128)S(1)} copy-done((f32[2,1024]{1,0:T(2,128)S(1)}, f32[2,1024]{1,0:T(2,128)}, u32[]{:S(2)}) %copy-start.3) | copy-done | bytes 8216
  4.1 0.0 copy-start.4
  4.1 0.7 %copy-done.4 = f32[2,1024]{1,0:T(2,128)S(1)} copy-done((f32[2,1024]{1,0:T(2,128)S(1)}, f32[2,1024]{1,0:T(2,128)}, u32[]{:S(2)}) %copy-start.4) | copy-done | bytes 8216
  4.8 0.0 copy-start.5
  4.8 0.7 %copy-done.5 = f32[2,1024]{1,0:T(2,128)S(1)} copy-done((f32[2,1024]{1,0:T(2,128)S(1)}, f32[2,1024]{1,0:T(2,128)}, u32[]{:S(2)}) %copy-start.5) | copy-done | bytes 8216
  5.5 0.0 copy-start.6
  5.5 0.7 %copy-done.6 = f32[1024]{0:T(1024)S(1)} copy-done((f32[1024]{0:T(1024)S(1)}, f32[1024]{0:T(1024)}, u32[]{:S(2)}) %copy-start.6) | copy-done | bytes 4120
  6.2 0.0 copy-start.7
  6.2 0.7 %copy-done.7 = s32[1,8]{1,0:T(1,128)S(1)} copy-done((s32[1,8]{1,0:T(1,128)S(1)}, s32[1,8]{1,0:T(1,128)}, u32[]{:S(2)}) %copy-start.7) | copy-done | bytes 56
  6.8 31.9 %hyena_modal_scan.1 = bf16[1,128,4096]{2,1,0:T(8,128)(2,1)S(1)} custom-call(bf16[3,1,128,4096]{3,2,1,0:T(8,128)(2,1)S(1)} %copy-done, f32[3,3,1024]{2,1,0:T(4,128)S(1)} %copy-done.1, f32[2,1024]{1,0:T(2,128)S(1)} %copy-done.2, f32[2,1024]{1,0:T(2,128)S(1)} %copy-done.3, f32[2,1024]{1,0:T(2,128)S(1)} %copy-done.4, f32[2,1024]{1,0:T(2,128)S(1)} %copy-done.5, ...), custom_call_target="tpu_custom_call" | custom-call | tf_op jit(solution)/shard_map/hyena_modal_scan/pallas_call | solution.py:464
  38.7 1.0 %copy.10 = bf16[1,128,4096]{2,1,0:T(8,128)(2,1)} copy(bf16[1,128,4096]{2,1,0:T(8,128)(2,1)S(1)} %hyena_modal_scan.1) | data formatting | bytes 2097152
Async XLA Ops:
  0.0 1.9 %copy-start = (bf16[3,1,128,4096]{3,2,1,0:T(8,128)(2,1)S(1)}, bf16[3,1,128,4096]{3,2,1,0:T(8,128)(2,1)}, u32[]{:S(2)}) copy-start(bf16[3,1,128,4096]{3,2,1,0:T(8,128)(2,1)} %streams_hbm.1) | copy-start | bytes 9437188
  1.9 0.8 %copy-start.1 = (f32[3,3,1024]{2,1,0:T(4,128)S(1)}, f32[3,3,1024]{2,1,0:T(4,128)}, u32[]{:S(2)}) copy-start(f32[3,3,1024]{2,1,0:T(4,128)} %taps_hbm.1) | copy-start | bytes 110596
  2.7 0.7 %copy-start.2 = (f32[2,1024]{1,0:T(2,128)S(1)}, f32[2,1024]{1,0:T(2,128)}, u32[]{:S(2)}) copy-start(f32[2,1024]{1,0:T(2,128)} %decay_hbm.1) | copy-start | bytes 24580
  3.4 0.7 %copy-start.3 = (f32[2,1024]{1,0:T(2,128)S(1)}, f32[2,1024]{1,0:T(2,128)}, u32[]{:S(2)}) copy-start(f32[2,1024]{1,0:T(2,128)} %angle_hbm.1) | copy-start | bytes 24580
  4.1 0.7 %copy-start.4 = (f32[2,1024]{1,0:T(2,128)S(1)}, f32[2,1024]{1,0:T(2,128)}, u32[]{:S(2)}) copy-start(f32[2,1024]{1,0:T(2,128)} %resr_hbm.1) | copy-start | bytes 24580
  4.8 0.7 %copy-start.5 = (f32[2,1024]{1,0:T(2,128)S(1)}, f32[2,1024]{1,0:T(2,128)}, u32[]{:S(2)}) copy-start(f32[2,1024]{1,0:T(2,128)} %resi_hbm.1) | copy-start | bytes 24580
  5.5 0.7 %copy-start.6 = (f32[1024]{0:T(1024)S(1)}, f32[1024]{0:T(1024)}, u32[]{:S(2)}) copy-start(f32[1024]{0:T(1024)} %param.14) | copy-start | bytes 12292
  6.2 0.7 %copy-start.7 = (s32[1,8]{1,0:T(1,128)S(1)}, s32[1,8]{1,0:T(1,128)}, u32[]{:S(2)}) copy-start(s32[1,8]{1,0:T(1,128)} %starts_hbm.1) | copy-start | bytes 100

commit v2 on v1

--- a/solution.py
+++ b/solution.py
@@ -40,10 +40,13 @@
     resi_hbm,
     skip_hbm,
     starts_hbm,
-    out_hbm,
+    out,
     xbuf,
     hsend,
     hrecv,
+    xs,
+    ends,
+    obuf,
     taps_v,
     decay_v,
     angle_v,
@@ -59,6 +62,7 @@
     perm_out,
     m_keep,
     m_tail,
+    m_head,
     m_first,
     m_scan,
     m_dev,
@@ -74,7 +78,6 @@
     r2,
     back,
     inflow,
-    obuf,
     in_sem,
     x_sem,
     pa_send,
@@ -90,6 +93,7 @@
     s3_send,
     s3_recv,
     o_sem,
+    known,
 ):
     n_z = n_seq // plane
     width = plane * LANES
@@ -106,15 +110,43 @@
     x_peer = [None] + [((me_x + n_dp - o) % n_dp, me) for o in offsets[1:]]
     q_rank = [(me_q + k) % plane for k in range(1, plane)]
     q_peer = [(me_x, me_z * plane + r) for r in q_rank]
-    z_peer = [(me_x, ((me_z + k) % n_z) * plane + me_q) for k in range(1, n_z)]
+    z_later = [(me_x, (me_z + k) % n_z * plane + me_q) for k in range(1, n_z)]
     after = (me_x, (me + 1) % n_seq)
     before = (me_x, (me + n_seq - 1) % n_seq)
     block = [(me_x + o) % n_dp for o in offsets]
 
+    def z_at(shift):
+        return (me_x, (me_z + shift + n_z) % n_z * plane + me_q)
+
+    def either(shift):
+        return [(me_z >= shift, z_at(-shift)), (me_z + shift < n_z, z_at(shift))]
+
     barrier = pltpu.get_barrier_semaphore()
-    peers = x_peer[1:] + q_peer + z_peer + [after, before]
-    for peer in peers:
+    greeted = jnp.int32(0)
+    for peer in x_peer[1:] + q_peer:
         pl.semaphore_signal(barrier, inc=1, device_id=peer, device_id_type=MESH)
+        greeted += 1
+    for near_by, peer in either(1) + [(me > 0, before), (me + 1 < n_seq, after)]:
+        greeted += jnp.where(near_by, 1, 0)
+
+        @pl.when(near_by)
+        def _():
+            pl.semaphore_signal(barrier, inc=1, device_id=peer, device_id_type=MESH)
+
+    rounds = [d for d in (1, 2, 4, 8, 16) if d < n_z - 1]
+
+    def tell(n):
+        for there, peer in either(rounds[n]):
+
+            @pl.when(there)
+            def _():
+                pl.semaphore_signal(known.at[n], inc=1, device_id=peer, device_id_type=MESH)
+
+    def learn(n):
+        count = jnp.int32(0)
+        for there, _ in either(rounds[n]):
+            count += jnp.where(there, 1, 0)
+        pl.semaphore_wait(known.at[n], count)
 
     loads = [
         pltpu.make_async_copy(a, b, in_sem.at[n])
@@ -139,16 +171,9 @@
         copy.start()
         x_loads.append(copy)
 
-    lines = TOK + 16
-    row = iota((lines, lines), 0)
-    col = iota((lines, lines), 1)
-    place = (row % CHUNKS) * STEPS + row // CHUNKS - 2
-    has_before = jnp.where(me > 0, 1, 0)
-    for s in range(3):
-        pick = jnp.where(place >= 0, place, jnp.where(has_before > 0, TOK + 2 * s + 2 + place, -1))
-        perm_in[s] = jnp.where(col == pick, 1.0, 0.0).astype(BF16)
     row = iota((TOK, TOK), 0)
     col = iota((TOK, TOK), 1)
+    perm_in[...] = jnp.where(col == (row % CHUNKS) * STEPS + row // CHUNKS, 1.0, 0.0).astype(BF16)
     perm_out[...] = jnp.where(col == (row % STEPS) * CHUNKS + row // STEPS, 1.0, 0.0).astype(BF16)
 
     for copy in loads[:6]:
@@ -175,37 +200,38 @@
     par_b[0, 3 * plane : 5 * plane, :] = norm * raw[2]
     par_b[0, 5 * plane : 7 * plane, :] = norm * raw[3]
 
-    row = iota((16, 16), 0)
-    col = iota((16, 16), 1)
-    for j in range(n_dp):
-        x_loads[j].wait()
-        for n in range(width // 256):
-            lane = slice(n * 256, (n + 1) * 256)
-            rim = jnp.zeros((16, 256), F32)
-            for s in range(3):
-                pick = jnp.where((row // 2 == s) & (col == 14 + row % 2), 1.0, 0.0).astype(BF16)
-                rim += jnp.dot(pick, xbuf[j, s, TOK - 16 :, lane], preferred_element_type=F32)
-            hsend[j, :, lane] = rim.astype(BF16)
-
-    pl.semaphore_wait(barrier, len(peers))
-
-    sends = []
-
-    def send(source, target, send_sem, recv_sem, device):
-        copy = pltpu.make_async_remote_copy(
+    @pl.when(me == 0)
+    def _():
+        hrecv[...] = jnp.zeros_like(hrecv)
+
+    pl.semaphore_wait(barrier, greeted)
+
+    def remote(source, target, send_sem, recv_sem, device):
+        return pltpu.make_async_remote_copy(
             src_ref=source, dst_ref=target, send_sem=send_sem, recv_sem=recv_sem, device_id=device, device_id_type=MESH
         )
-        copy.start()
-        sends.append(copy)
-        return copy
-
-    a_copies = [None] + [
-        send(par_a.at[0], par_a.at[j], pa_send.at[j], pa_recv.at[j], x_peer[j]) for j in range(1, n_dp)
-    ]
-    h_copies = [send(hsend.at[j], hrecv.at[j], h_send.at[j], h_recv.at[j], after) for j in range(n_dp)]
-    b_copies = [None] + [
-        send(par_b.at[0], par_b.at[j], pb_send.at[j], pb_recv.at[j], x_peer[j]) for j in range(1, n_dp)
-    ]
+
+    def send_a(j):
+        return remote(par_a.at[0], par_a.at[j], pa_send.at[j - 1], pa_recv.at[j - 1], x_peer[j])
+
+    def send_b(j):
+        return remote(par_b.at[0], par_b.at[j], pb_send.at[j - 1], pb_recv.at[j - 1], x_peer[j])
+
+    def send_h(j):
+        return remote(hsend.at[j], hrecv.at[j], h_send.at[j], h_recv.at[j], after)
+
+    for j in range(1, n_dp):
+        send_a(j).start()
+    if rounds:
+        tell(0)
+    for j in range(n_dp):
+        x_loads[j].wait()
+        for s in range(3):
+            hsend[j, 2 * s : 2 * s + 2, :] = xbuf[j, s, TOK - 16 :, :].astype(F32)[14:16]
+
+        @pl.when(me + 1 < n_seq)
+        def _():
+            send_h(j).start()
 
     loads[6].wait()
     starts = [starts_s[0, d] for d in range(starts_s.shape[1])]
@@ -223,7 +249,11 @@
     for k in range(STEPS):
         here = chunk * STEPS + k
         m_keep[k] = free(here, here + 1, near)
-        m_tail[k] = free(here + 1, chunk * STEPS + STEPS, near)
+        tail = free(here + 1, chunk * STEPS + STEPS, near)
+        if k < 2:
+            m_head[k] = jnp.where(chunk == 0, tail, zero)
+            tail = jnp.where(chunk == 0, zero, tail)
+        m_tail[k] = tail
         m_first[k] = free(jnp.zeros_like(here), here + 1, near)
     for n, shift in enumerate((1, 2, 4)):
         reach = free((chunk - shift + 1) * STEPS, (chunk + 1) * STEPS, near)
@@ -232,56 +262,103 @@
     m_dev[0] = free(first_of_plane + chunk * TOK, first_of_plane + (chunk + 1) * TOK, starts)
     m_dev[1] = free(chunk * plane * TOK, (chunk + 1) * plane * TOK, starts)
 
+    has_before = jnp.where(me > 0, 1.0, 0.0).astype(F32)
+    reach_near = 2 * rounds[1] if len(rounds) > 1 else n_z - 1
+    near_planes = [k for k in range(1, n_z) if k <= reach_near]
+    far_planes = [k for k in range(1, n_z) if k > reach_near]
     n_rows = 2 * plane
     log_plane = plane.bit_length() - 1
 
-    def filters(j, s, i, source, base, x):
+    def filters(j, i, source, base, x):
         c = [rows(source.at[j], (base + k) * plane + i) for k in range(3)]
+        x = [pltpu.roll(x[STEPS - 2], 1, axis=0), pltpu.roll(x[STEPS - 1], 1, axis=0)] + x
         return [c[0] * x[k + 2] + c[1] * x[k + 1] + c[2] * x[k] for k in range(STEPS)]
+
+    def first_two(j, s, i, source, base, x):
+        c = [rows(source.at[j], (base + k) * plane + i) for k in range(3)]
+        lane = pl.ds(pl.multiple_of(i * LANES, LANES), LANES)
+        older = rows(hrecv.at[j, :, lane], 2 * s) * has_before
+        old = rows(hrecv.at[j, :, lane], 2 * s + 1) * has_before
+        return [c[0] * x[0] + c[1] * old + c[2] * older, c[0] * x[1] + c[1] * x[0] + c[2] * old]
 
     def permuted(j, s, i2):
         lane = pl.ds(pl.multiple_of(i2 * 256, 256), 256)
-        operand = jnp.concatenate([xbuf[j, s, :, lane], hrecv[j, :, lane]], axis=0)
-        return jnp.dot(perm_in[s], operand, preferred_element_type=F32)
-
-    def half(x, h):
-        return [x[8 * g : 8 * g + 8, h * LANES : (h + 1) * LANES] for g in range(STEPS + 2)]
-
-    def states(j):
+        return jnp.dot(perm_in[...], xbuf[j, s, :, lane], preferred_element_type=F32)
+
+    def permute(j):
+        for i2 in range(width // 256):
+            for s in range(2):
+                x = permuted(j, s, i2)
+                xs[j, s, 2 * i2] = x[:, :LANES]
+                xs[j, s, 2 * i2 + 1] = x[:, LANES:]
+
+    def steps_of(ref, count=STEPS):
+        return [ref[8 * k : 8 * k + 8, :] for k in range(count)]
+
+    def powers(j):
         pr = par_a[j, 6 * plane : 8 * plane, :]
         pi = par_a[j, 8 * plane : 10 * plane, :]
         qr, qi = pr, pi
+        tr, ti = pr, pi
         slot = 0
         for n in range(7 + log_plane):
             qr, qi = qr * qr - qi * qi, 2.0 * qr * qi
+            if n == 0:
+                tr, ti = qr, qi
+            elif n < 3:
+                tr, ti = cmul(tr, ti, qr, qi)
             if n + 1 in (4, 5, 6, 7, 7 + log_plane):
                 derived[j, slot * n_rows : (slot + 1) * n_rows, :] = qr
                 derived[j, (slot + 1) * n_rows : (slot + 2) * n_rows, :] = qi
                 slot += 2
         derived[j, 10 * n_rows : 11 * n_rows, :] = 2.0 * pr
         derived[j, 11 * n_rows : 12 * n_rows, :] = pr * pr + pi * pi
-
-        @pl.loop(0, width // 256)
+        derived[j, 12 * n_rows : 13 * n_rows, :] = tr
+        derived[j, 13 * n_rows : 14 * n_rows, :] = ti
+        tr, ti = cmul(tr, ti, pr, pi)
+        derived[j, 14 * n_rows : 15 * n_rows, :] = tr
+        derived[j, 15 * n_rows : 16 * n_rows, :] = ti
+
+    def products(j):
+        powers(j)
+
+        @pl.loop(0, plane // 2)
         def _(i2):
-            x0 = permuted(j, 0, i2)
-            x1 = permuted(j, 1, i2)
-            for h in range(2):
-                i = 2 * i2 + h
-                f0 = filters(j, 0, i, par_a, 0, half(x0, h))
-                f1 = filters(j, 1, i, par_a, 3, half(x1, h))
-                v = [a * b for a, b in zip(f0, f1)]
+            for i in (2 * i2, 2 * i2 + 1):
+                f0 = filters(j, i, par_a, 0, steps_of(xs.at[j, 0, i]))
+                f1 = filters(j, i, par_a, 3, steps_of(xs.at[j, 1, i]))
+                masked = []
                 for k in range(STEPS):
-                    vbuf[j, i, 8 * k : 8 * k + 8, :] = v[k]
-                masked = [v[k] * m_tail[k] for k in range(STEPS)]
+                    v = f0[k] * f1[k]
+                    vbuf[j, i, 8 * k : 8 * k + 8, :] = v
+                    masked.append(v * m_tail[k])
                 for m in range(2):
                     r = 2 * i + m
                     a1 = rows(derived.at[j], 10 * n_rows + r)
                     a2 = rows(derived.at[j], 11 * n_rows + r)
-                    b1, b2 = masked[0], zero
-                    for k in range(1, STEPS):
+                    b2, b1 = masked[0], a1 * masked[0] + masked[1]
+                    for k in range(2, STEPS):
                         b1, b2 = a1 * b1 + (masked[k] - a2 * b2), b1
-                    er = b1 - rows(par_a.at[j], 6 * plane + r) * b2
-                    ei = rows(par_a.at[j], 8 * plane + r) * b2
+                    ends[j, i, 16 * m : 16 * m + 8, :] = b1 - rows(par_a.at[j], 6 * plane + r) * b2
+                    ends[j, i, 16 * m + 8 : 16 * m + 16, :] = rows(par_a.at[j], 8 * plane + r) * b2
+
+    def states(j):
+        @pl.loop(0, plane // 2)
+        def _(i2):
+            for i in (2 * i2, 2 * i2 + 1):
+                f0 = first_two(j, 0, i, par_a, 0, steps_of(xs.at[j, 0, i], 2))
+                f1 = first_two(j, 1, i, par_a, 3, steps_of(xs.at[j, 1, i], 2))
+                v = [f0[k] * f1[k] for k in range(2)]
+                for k in range(2):
+                    vbuf[j, i, 8 * k : 8 * k + 8, :] = jnp.where(
+                        chunk == 0, v[k], vbuf[j, i, 8 * k : 8 * k + 8, :]
+                    )
+                v = [v[k] * m_head[k] for k in range(2)]
+                for m in range(2):
+                    r = 2 * i + m
+                    p14, q14, p15, q15 = [rows(derived.at[j], (12 + n) * n_rows + r) for n in range(4)]
+                    er = ends[j, i, 16 * m : 16 * m + 8, :] + (v[0] * p15 + v[1] * p14)
+                    ei = ends[j, i, 16 * m + 8 : 16 * m + 16, :] + (v[0] * q15 + v[1] * q14)
                     for n, shift in enumerate((1, 2, 4)):
                         reach = m_scan[n]
                         kr = reach * rows(derived.at[j], 2 * n * n_rows + r)
@@ -298,14 +375,29 @@
 
     def gather_plane(j):
         r1[j, me_q] = state[j, me_q]
-        return [
-            send(state.at[j, q_rank[n]], r1.at[j, me_q], s1_send.at[j, n], s1_recv.at[j, n], q_peer[n])
-            for n in range(plane - 1)
-        ]
-
-    def combine_plane(j, copies):
-        for copy in copies:
-            copy.wait_recv()
+        for n in range(plane - 1):
+            remote(state.at[j, q_rank[n]], r1.at[j, me_q], s1_send.at[j], s1_recv.at[j], q_peer[n]).start()
+
+    def whole_1(j):
+        others = pl.ds(0, plane - 1)
+        return remote(state.at[j, others], r1.at[j, others], s1_send.at[j], s1_recv.at[j], q_peer[0])
+
+    def whole_3(j):
+        others = pl.ds(0, plane - 1)
+        return remote(back.at[j, others], inflow.at[j, others], s3_send.at[j], s3_recv.at[j], q_peer[0])
+
+    def send_2(j, k):
+        return remote(total.at[j], r2.at[j, me_z], s2_send.at[j, k - 1], s2_recv.at[j, k - 1], z_later[k - 1])
+
+    def later_planes(j, distances, act):
+        for k in distances:
+
+            @pl.when(me_z + k < n_z)
+            def _():
+                act(send_2(j, k))
+
+    def combine_plane(j):
+        whole_1(j).wait_recv()
         pr = derived[j, pl.ds(6 * n_rows + 2 * me_q, 2), :]
         pi = derived[j, pl.ds(7 * n_rows + 2 * me_q, 2), :]
         run_r = jnp.zeros((2, LANES), F32)
@@ -319,14 +411,15 @@
             run_i = ai + r1[j, e, 2:4, :]
         total[j, 0:2, :] = run_r
         total[j, 2:4, :] = run_i
-        r2[j, me_z] = total[j]
-        return [
-            send(total.at[j], r2.at[j, me_z], s2_send.at[j, n], s2_recv.at[j, n], z_peer[n]) for n in range(n_z - 1)
-        ]
-
-    def combine_all(j, copies):
-        for copy in copies:
-            copy.wait_recv()
+        later_planes(j, near_planes, lambda copy: copy.start())
+
+    def combine_all(j):
+        for k in range(1, n_z):
+
+            @pl.when(me_z >= k)
+            def _():
+                send_2(j, k).wait_recv()
+
         pr = derived[j, pl.ds(8 * n_rows + 2 * me_q, 2), :]
         pi = derived[j, pl.ds(9 * n_rows + 2 * me_q, 2), :]
         run_r = jnp.zeros((2, LANES), F32)
@@ -345,10 +438,8 @@
             keep = m_dev[0, e : e + 1, :]
             run_r, run_i = cmul(pr * keep, pi * keep, run_r, run_i)
         inflow[j, me_q] = back[j, me_q]
-        return [
-            send(back.at[j, q_rank[n]], inflow.at[j, me_q], s3_send.at[j, n], s3_recv.at[j, n], q_peer[n])
-            for n in range(plane - 1)
-        ]
+        for n in range(plane - 1):
+            remote(back.at[j, q_rank[n]], inflow.at[j, me_q], s3_send.at[j], s3_recv.at[j], q_peer[n]).start()
 
     def response(j):
         @pl.loop(0, width // 256)
@@ -356,7 +447,11 @@
             x2 = permuted(j, 2, i2)
             for h in range(2):
                 i = 2 * i2 + h
-                gate = filters(j, 2, i, par_b, 0, half(x2, h))
+                x = [x2[8 * k : 8 * k + 8, h * LANES : (h + 1) * LANES] for k in range(STEPS)]
+                gate = filters(j, i, par_b, 0, x)
+                head = first_two(j, 2, i, par_b, 0, x)
+                for k in range(2):
+                    gate[k] = jnp.where(chunk == 0, head[k], gate[k])
                 skip = rows(par_b.at[j], 7 * plane + i)
                 v = [vbuf[j, i, 8 * k : 8 * k + 8, :] for k in range(STEPS)]
                 y = [skip * v[k] for k in range(STEPS)]
@@ -388,12 +483,10 @@
                     gr[j, i, 8 * k : 8 * k + 8, :] = gate[k] * y[k]
                     gm[j, i, 8 * k : 8 * k + 8, :] = gate[k] * m_first[k]
 
-    def finish(j, copies):
-        for copy in copies:
-            copy.wait_recv()
-
-        @pl.loop(0, width // 256)
-        def _(i2):
+    def finish(j):
+        whole_3(j).wait_recv()
+
+        for i2 in range(width // 256):
             halves = []
             for h in range(2):
                 i = 2 * i2 + h
@@ -421,33 +514,61 @@
                     )
                 )
             mixed = jnp.concatenate(halves, axis=1).astype(BF16)
-            lane = pl.ds(pl.multiple_of(i2 * 256, 256), 256)
-            obuf[j, :, lane] = jnp.dot(perm_out[...], mixed, preferred_element_type=F32).astype(BF16)
-
+            obuf[j, :, i2 * 256 : i2 * 256 + 256] = jnp.dot(perm_out[...], mixed, preferred_element_type=F32).astype(BF16)
         columns = pl.ds(pl.multiple_of(block[j] * width, width), width)
-        copy = pltpu.make_async_copy(obuf.at[j], out_hbm.at[0, :, columns], o_sem.at[j])
+        copy = pltpu.make_async_copy(obuf.at[j], out.at[0, :, columns], o_sem.at[j])
         copy.start()
         return copy
 
-    one_copies = []
+    for j in range(n_dp):
+        permute(j)
+    products(0)
+    if rounds:
+        learn(0)
+    if len(rounds) > 1:
+        tell(1)
+    for j in range(1, n_dp):
+        send_a(j).wait_recv()
+        products(j)
+    for j in range(1, n_dp):
+        send_b(j).start()
+    for j in range(n_dp):
+
+        @pl.when(me > 0)
+        def _():
+            send_h(j).wait_recv()
+
+        states(j)
+        gather_plane(j)
+    if len(rounds) > 1:
+        learn(1)
+    if len(rounds) > 2:
+        tell(2)
+    response(0)
+    for j in range(n_dp):
+        combine_plane(j)
+    for j in range(1, n_dp):
+        send_b(j).wait_recv()
+        response(j)
+    for j in range(n_dp):
+        combine_all(j)
+    if far_planes:
+        learn(2)
+    for j in range(n_dp):
+        later_planes(j, far_planes, lambda copy: copy.start())
+    stores = [finish(j) for j in range(n_dp)]
     for j in range(n_dp):
         if j:
-            a_copies[j].wait_recv()
-        h_copies[j].wait_recv()
-        states(j)
-        one_copies.append(gather_plane(j))
-    two_copies = []
-    for j in range(n_dp):
-        two_copies.append(combine_plane(j, one_copies[j]))
-        if j:
-            b_copies[j].wait_recv()
-        if j < n_dp - 1:
-            response(j)
-    response(n_dp - 1)
-    three_copies = [combine_all(j, two_copies[j]) for j in range(n_dp)]
-    stores = [finish(j, three_copies[j]) for j in range(n_dp)]
-    for copy in sends:
-        copy.wait_send()
+            send_a(j).wait_send()
+            send_b(j).wait_send()
+
+        @pl.when(me + 1 < n_seq)
+        def _():
+            send_h(j).wait_send()
+
+        whole_1(j).wait_send()
+        later_planes(j, range(1, n_z), lambda copy: copy.wait_send())
+        whole_3(j).wait_send()
     for copy in stores:
         copy.wait()
 
@@ -460,7 +581,6 @@
     vmem = pltpu.VMEM
     dma = pltpu.SemaphoreType.DMA
     anywhere = pl.BlockSpec(memory_space=pl.ANY)
-    lines = TOK + 16
     return pl.pallas_call(
         functools.partial(kernel, n_dp, n_seq, plane),
         out_shape=jax.ShapeDtypeStruct((1, TOK, streams.shape[3]), BF16),
@@ -468,8 +588,11 @@
         out_specs=anywhere,
         scratch_shapes=[
             vmem((n_dp, 3, TOK, width), BF16),
-            vmem((n_dp, 16, width), BF16),
-            vmem((n_dp, 16, width), BF16),
+            vmem((n_dp, 8, width), F32),
+            vmem((n_dp, 8, width), F32),
+            vmem((n_dp, 2, plane, TOK, LANES), F32),
+            vmem((n_dp, plane, 32, LANES), F32),
+            vmem((n_dp, TOK, width), BF16),
             vmem((3, 3, width), F32),
             vmem((2, width), F32),
             vmem((2, width), F32),
@@ -480,11 +603,12 @@
             pltpu.SMEM(doc_starts.shape, jnp.int32),
             vmem((n_dp, 10 * plane, LANES), F32),
             vmem((n_dp, 8 * plane, LANES), F32),
-            vmem((n_dp, 12 * n_rows, LANES), F32),
-            vmem((3, lines, lines), BF16),
+            vmem((n_dp, 16 * n_rows, LANES), F32),
+            vmem((TOK, TOK), BF16),
             vmem((TOK, TOK), BF16),
             vmem((STEPS, 8, LANES), F32),
             vmem((STEPS, 8, LANES), F32),
+            vmem((2, 8, LANES), F32),
             vmem((STEPS, 8, LANES), F32),
             vmem((3, 8, LANES), F32),
             vmem((2, 8, LANES), F32),
@@ -500,34 +624,39 @@
             vmem((n_dp, n_z, 4, LANES), F32),
             vmem((n_dp, plane, 4, LANES), F32),
             vmem((n_dp, plane, 4, LANES), F32),
-            vmem((n_dp, TOK, width), BF16),
             dma((7,)),
             dma((n_dp,)),
-            dma((n_dp,)),
-            dma((n_dp,)),
-            dma((n_dp,)),
-            dma((n_dp,)),
-            dma((n_dp,)),
-            dma((n_dp,)),
-            dma((n_dp, plane - 1)),
-            dma((n_dp, plane - 1)),
+            dma((n_dp - 1,)),
+            dma((n_dp - 1,)),
+            dma((n_dp - 1,)),
+            dma((n_dp - 1,)),
+            dma((n_dp,)),
+            dma((n_dp,)),
+            dma((n_dp,)),
+            dma((n_dp,)),
             dma((n_dp, n_z - 1)),
             dma((n_dp, n_z - 1)),
-            dma((n_dp, plane - 1)),
-            dma((n_dp, plane - 1)),
-            dma((n_dp,)),
+            dma((n_dp,)),
+            dma((n_dp,)),
+            dma((n_dp,)),
+            pltpu.SemaphoreType.REGULAR((3,)),
         ],
         compiler_params=pltpu.CompilerParams(collective_id=0, has_side_effects=True, vmem_limit_bytes=48 * 2**20),
         name="hyena_modal_scan",
     )(
-        streams,
-        short_filter,
-        decay_rate,
-        pole_angle,
-        residue_re,
-        residue_im,
-        skip_gain.reshape(1, width),
-        doc_starts,
+        *[
+            pltpu.with_memory_space_constraint(a, pltpu.HBM)
+            for a in (
+                streams,
+                short_filter,
+                decay_rate,
+                pole_angle,
+                residue_re,
+                residue_im,
+                skip_gain.reshape(1, width),
+                doc_starts,
+            )
+        ]
     )
 
 

time: 40.1 us -> 25.5 us (0.64)
  the two profiles are of different devices: /device:TPU:1 before, /device:TPU:225 now
where the time goes in v2:
time: 25.5 us; the launch traced here: 25.4 us
  Pallas kernels  24.4 us (96%)
  local copies, waits for them, and re-layouts  0.97 us (4%)
    pallas_call x1, Pallas kernels, local(): pl.pallas_call(functools.partial(kernel, n_dp, n_seq, plane), out_shape=j...  24.4 us
    unnamed x1, local copies, waits for them, and re-layouts  0.97 us

profile of v2, /device:TPU:225, one launch (start us, length us, event | category | flops | bytes accessed | tf_op | source)
XLA Modules:
  0.0 25.4 jit_solution(17342709502112495500)
XLA Ops:
  0.0 24.4 %hyena_modal_scan.1 = bf16[1,128,4096]{2,1,0:T(8,128)(2,1)S(1)} custom-call(bf16[3,1,128,4096]{3,2,1,0:T(8,128)(2,1)} %streams_hbm.1, f32[3,3,1024]{2,1,0:T(4,128)} %taps_hbm.1, f32[2,1024]{1,0:T(2,128)} %decay_hbm.1, f32[2,1024]{1,0:T(2,128)} %angle_hbm.1, f32[2,1024]{1,0:T(2,128)} %resr_hbm.1, f32[2,1024]{1,0:T(2,128)} %resi_hbm.1, f32[1,1024]{1,0:T(1,128)} %bitcast.1, ...), custom_call_target="tpu_custom_call" | custom-call | tf_op jit(solution)/shard_map/hyena_modal_scan/pallas_call | solution.py:584
  24.4 1.0 %copy.10 = bf16[1,128,4096]{2,1,0:T(8,128)(2,1)} copy(bf16[1,128,4096]{2,1,0:T(8,128)(2,1)S(1)} %hyena_modal_scan.1) | data formatting | bytes 2097152

commit v3 on v2

--- a/solution.py
+++ b/solution.py
@@ -44,6 +44,8 @@
     xbuf,
     hsend,
     hrecv,
+    hsrc,
+    hrows,
     xs,
     ends,
     obuf,
@@ -164,12 +166,8 @@
     ]
     for copy in loads:
         copy.start()
-    x_loads = []
-    for j in range(n_dp):
-        columns = pl.ds(pl.multiple_of(block[j] * width, width), width)
-        copy = pltpu.make_async_copy(streams_hbm.at[:, 0, :, columns], xbuf.at[j], x_sem.at[j])
-        copy.start()
-        x_loads.append(copy)
+    x_load = pltpu.make_async_copy(streams_hbm.at[:, 0], xbuf, x_sem)
+    x_load.start()
 
     row = iota((TOK, TOK), 0)
     col = iota((TOK, TOK), 1)
@@ -204,6 +202,8 @@
     def _():
         hrecv[...] = jnp.zeros_like(hrecv)
 
+    hsrc[...] = jnp.zeros_like(hsrc)
+
     pl.semaphore_wait(barrier, greeted)
 
     def remote(source, target, send_sem, recv_sem, device):
@@ -217,21 +217,24 @@
     def send_b(j):
         return remote(par_b.at[0], par_b.at[j], pb_send.at[j - 1], pb_recv.at[j - 1], x_peer[j])
 
-    def send_h(j):
-        return remote(hsend.at[j], hrecv.at[j], h_send.at[j], h_recv.at[j], after)
-
     for j in range(1, n_dp):
         send_a(j).start()
     if rounds:
         tell(0)
-    for j in range(n_dp):
-        x_loads[j].wait()
-        for s in range(3):
-            hsend[j, 2 * s : 2 * s + 2, :] = xbuf[j, s, TOK - 16 :, :].astype(F32)[14:16]
-
-        @pl.when(me + 1 < n_seq)
-        def _():
-            send_h(j).start()
+    x_load.wait()
+    half = n_dp * width // 2
+    for s in range(3):
+        last = xbuf[s, TOK - 16 :, :].astype(F32)[14:16]
+        for h in range(2):
+            hsrc[8 * h + 2 * s : 8 * h + 2 * s + 2, :] = last[:, h * half : (h + 1) * half]
+    hsend[...] = hsrc[...].astype(BF16)
+
+    def send_h():
+        return remote(hsend, hrecv, h_send, h_recv, after)
+
+    @pl.when(me + 1 < n_seq)
+    def _():
+        send_h().start()
 
     loads[6].wait()
     starts = [starts_s[0, d] for d in range(starts_s.shape[1])]
@@ -262,7 +265,6 @@
     m_dev[0] = free(first_of_plane + chunk * TOK, first_of_plane + (chunk + 1) * TOK, starts)
     m_dev[1] = free(chunk * plane * TOK, (chunk + 1) * plane * TOK, starts)
 
-    has_before = jnp.where(me > 0, 1.0, 0.0).astype(F32)
     reach_near = 2 * rounds[1] if len(rounds) > 1 else n_z - 1
     near_planes = [k for k in range(1, n_z) if k <= reach_near]
     far_planes = [k for k in range(1, n_z) if k > reach_near]
@@ -276,14 +278,13 @@
 
     def first_two(j, s, i, source, base, x):
         c = [rows(source.at[j], (base + k) * plane + i) for k in range(3)]
-        lane = pl.ds(pl.multiple_of(i * LANES, LANES), LANES)
-        older = rows(hrecv.at[j, :, lane], 2 * s) * has_before
-        old = rows(hrecv.at[j, :, lane], 2 * s + 1) * has_before
+        older = rows(hrows.at[block[j] * plane + i], 2 * s)
+        old = rows(hrows.at[block[j] * plane + i], 2 * s + 1)
         return [c[0] * x[0] + c[1] * old + c[2] * older, c[0] * x[1] + c[1] * x[0] + c[2] * old]
 
     def permuted(j, s, i2):
-        lane = pl.ds(pl.multiple_of(i2 * 256, 256), 256)
-        return jnp.dot(perm_in[...], xbuf[j, s, :, lane], preferred_element_type=F32)
+        lane = pl.ds(pl.multiple_of(block[j] * width + i2 * 256, 256), 256)
+        return jnp.dot(perm_in[...], xbuf[s, :, lane], preferred_element_type=F32)
 
     def permute(j):
         for i2 in range(width // 256):
@@ -387,14 +388,18 @@
         return remote(back.at[j, others], inflow.at[j, others], s3_send.at[j], s3_recv.at[j], q_peer[0])
 
     def send_2(j, k):
-        return remote(total.at[j], r2.at[j, me_z], s2_send.at[j, k - 1], s2_recv.at[j, k - 1], z_later[k - 1])
-
-    def later_planes(j, distances, act):
+        return remote(total.at[j], r2.at[j, me_z], s2_send.at[j], s2_recv.at[j], z_later[k - 1])
+
+    def later_planes(j, distances):
         for k in distances:
 
             @pl.when(me_z + k < n_z)
             def _():
-                act(send_2(j, k))
+                send_2(j, k).start()
+
+    def whole_2(j, count):
+        those = pl.ds(0, count)
+        return remote(r2.at[j, those], r2.at[j, those], s2_send.at[j], s2_recv.at[j], z_later[0])
 
     def combine_plane(j):
         whole_1(j).wait_recv()
@@ -411,14 +416,14 @@
             run_i = ai + r1[j, e, 2:4, :]
         total[j, 0:2, :] = run_r
         total[j, 2:4, :] = run_i
-        later_planes(j, near_planes, lambda copy: copy.start())
+        later_planes(j, near_planes)
 
     def combine_all(j):
-        for k in range(1, n_z):
-
-            @pl.when(me_z >= k)
+        for count in range(1, n_z):
+
+            @pl.when(me_z == count)
             def _():
-                send_2(j, k).wait_recv()
+                whole_2(j, count).wait_recv()
 
         pr = derived[j, pl.ds(8 * n_rows + 2 * me_q, 2), :]
         pi = derived[j, pl.ds(9 * n_rows + 2 * me_q, 2), :]
@@ -529,15 +534,23 @@
         tell(1)
     for j in range(1, n_dp):
         send_a(j).wait_recv()
+        if j == n_dp - 1:
+            for n in range(1, n_dp):
+                send_b(n).start()
         products(j)
-    for j in range(1, n_dp):
-        send_b(j).start()
-    for j in range(n_dp):
-
-        @pl.when(me > 0)
-        def _():
-            send_h(j).wait_recv()
-
+        if j == 1:
+
+            @pl.when(me > 0)
+            def _():
+                send_h().wait_recv()
+
+            tiles = half // LANES
+            for t in range(tiles):
+                both = hrecv[:, t * LANES : (t + 1) * LANES].astype(F32)
+                hrows[t] = both[:8]
+                hrows[tiles + t] = both[8:]
+            states(0)
+            gather_plane(0)
         states(j)
         gather_plane(j)
     if len(rounds) > 1:
@@ -555,19 +568,24 @@
     if far_planes:
         learn(2)
     for j in range(n_dp):
-        later_planes(j, far_planes, lambda copy: copy.start())
+        later_planes(j, far_planes)
     stores = [finish(j) for j in range(n_dp)]
+
+    @pl.when(me + 1 < n_seq)
+    def _():
+        send_h().wait_send()
+
     for j in range(n_dp):
         if j:
             send_a(j).wait_send()
             send_b(j).wait_send()
-
-        @pl.when(me + 1 < n_seq)
-        def _():
-            send_h(j).wait_send()
-
         whole_1(j).wait_send()
-        later_planes(j, range(1, n_z), lambda copy: copy.wait_send())
+        for count in range(1, n_z):
+
+            @pl.when(me_z + count == n_z - 1)
+            def _():
+                whole_2(j, count).wait_send()
+
         whole_3(j).wait_send()
     for copy in stores:
         copy.wait()
@@ -587,9 +605,11 @@
         in_specs=[anywhere] * 8,
         out_specs=anywhere,
         scratch_shapes=[
-            vmem((n_dp, 3, TOK, width), BF16),
-            vmem((n_dp, 8, width), F32),
-            vmem((n_dp, 8, width), F32),
+            vmem((3, TOK, n_dp * width), BF16),
+            vmem((16, n_dp * width // 2), BF16),
+            vmem((16, n_dp * width // 2), BF16),
+            vmem((16, n_dp * width // 2), F32),
+            vmem((n_dp * plane, 8, LANES), F32),
             vmem((n_dp, 2, plane, TOK, LANES), F32),
             vmem((n_dp, plane, 32, LANES), F32),
             vmem((n_dp, TOK, width), BF16),
@@ -625,17 +645,17 @@
             vmem((n_dp, plane, 4, LANES), F32),
             vmem((n_dp, plane, 4, LANES), F32),
             dma((7,)),
-            dma((n_dp,)),
+            dma(()),
             dma((n_dp - 1,)),
             dma((n_dp - 1,)),
             dma((n_dp - 1,)),
             dma((n_dp - 1,)),
+            dma(()),
+            dma(()),
             dma((n_dp,)),
             dma((n_dp,)),
             dma((n_dp,)),
             dma((n_dp,)),
-            dma((n_dp, n_z - 1)),
-            dma((n_dp, n_z - 1)),
             dma((n_dp,)),
             dma((n_dp,)),
             dma((n_dp,)),

time: 25.5 us -> 24.3 us (0.953)
  Pallas kernels: 24.4 us -> 23.2 us
    pallas_call x1, Pallas kernels: 24.4 us -> 23.2 us  [local(): pl.pallas_call(functools.partial(kernel, n_dp, n_seq, plane), out_shape=j...]
where the time goes in v3:
time: 24.3 us; the launch traced here: 24.2 us
  Pallas kernels  23.2 us (95%)
  local copies, waits for them, and re-layouts  0.97 us (4%)
    pallas_call x1, Pallas kernels, local(): pl.pallas_call(functools.partial(kernel, n_dp, n_seq, plane), out_shape=j...  23.2 us
    unnamed x1, local copies, waits for them, and re-layouts  0.97 us

profile of v3, /device:TPU:225, one launch (start us, length us, event | category | flops | bytes accessed | tf_op | source)
XLA Modules:
  0.0 24.2 jit_solution(18267203616060931384)
XLA Ops:
  0.0 23.2 %hyena_modal_scan.1 = bf16[1,128,4096]{2,1,0:T(8,128)(2,1)S(1)} custom-call(bf16[3,1,128,4096]{3,2,1,0:T(8,128)(2,1)} %streams_hbm.1, f32[3,3,1024]{2,1,0:T(4,128)} %taps_hbm.1, f32[2,1024]{1,0:T(2,128)} %decay_hbm.1, f32[2,1024]{1,0:T(2,128)} %angle_hbm.1, f32[2,1024]{1,0:T(2,128)} %resr_hbm.1, f32[2,1024]{1,0:T(2,128)} %resi_hbm.1, f32[1,1024]{1,0:T(1,128)} %bitcast.1, ...), custom_call_target="tpu_custom_call" | custom-call | tf_op jit(solution)/shard_map/hyena_modal_scan/pallas_call | solution.py:602
  23.3 1.0 %copy.10 = bf16[1,128,4096]{2,1,0:T(8,128)(2,1)} copy(bf16[1,128,4096]{2,1,0:T(8,128)(2,1)S(1)} %hyena_modal_scan.1) | data formatting | bytes 2097152

commit v4 on v3

--- a/solution.py
+++ b/solution.py
@@ -120,35 +120,34 @@
     def z_at(shift):
         return (me_x, (me_z + shift + n_z) % n_z * plane + me_q)
 
-    def either(shift):
-        return [(me_z >= shift, z_at(-shift)), (me_z + shift < n_z, z_at(shift))]
-
     barrier = pltpu.get_barrier_semaphore()
-    greeted = jnp.int32(0)
     for peer in x_peer[1:] + q_peer:
         pl.semaphore_signal(barrier, inc=1, device_id=peer, device_id_type=MESH)
-        greeted += 1
-    for near_by, peer in either(1) + [(me > 0, before), (me + 1 < n_seq, after)]:
+    greeted = jnp.int32(len(x_peer) - 1 + len(q_peer)) + me_z
+    for near_by, peer in [(me > 0, before), (me + 1 < n_seq, after)]:
         greeted += jnp.where(near_by, 1, 0)
 
         @pl.when(near_by)
         def _():
             pl.semaphore_signal(barrier, inc=1, device_id=peer, device_id_type=MESH)
 
-    rounds = [d for d in (1, 2, 4, 8, 16) if d < n_z - 1]
-
-    def tell(n):
-        for there, peer in either(rounds[n]):
-
-            @pl.when(there)
+    for k in range(1, n_z):
+
+        @pl.when(me_z + k < n_z)
+        def _():
+            pl.semaphore_signal(barrier, inc=1, device_id=z_at(k), device_id_type=MESH)
+
+    def tell_earlier():
+        for k in range(1, n_z):
+
+            @pl.when(me_z >= k)
             def _():
-                pl.semaphore_signal(known.at[n], inc=1, device_id=peer, device_id_type=MESH)
-
-    def learn(n):
-        count = jnp.int32(0)
-        for there, _ in either(rounds[n]):
-            count += jnp.where(there, 1, 0)
-        pl.semaphore_wait(known.at[n], count)
+                pl.semaphore_signal(known, inc=1, device_id=z_at(-k), device_id_type=MESH)
+
+    def learn_later():
+        @pl.when(me_z < n_z - 1)
+        def _():
+            pl.semaphore_wait(known, n_z - 1 - me_z)
 
     loads = [
         pltpu.make_async_copy(a, b, in_sem.at[n])
@@ -219,8 +218,7 @@
 
     for j in range(1, n_dp):
         send_a(j).start()
-    if rounds:
-        tell(0)
+    tell_earlier()
     x_load.wait()
     half = n_dp * width // 2
     for s in range(3):
@@ -265,9 +263,6 @@
     m_dev[0] = free(first_of_plane + chunk * TOK, first_of_plane + (chunk + 1) * TOK, starts)
     m_dev[1] = free(chunk * plane * TOK, (chunk + 1) * plane * TOK, starts)
 
-    reach_near = 2 * rounds[1] if len(rounds) > 1 else n_z - 1
-    near_planes = [k for k in range(1, n_z) if k <= reach_near]
-    far_planes = [k for k in range(1, n_z) if k > reach_near]
     n_rows = 2 * plane
     log_plane = plane.bit_length() - 1
 
@@ -288,7 +283,7 @@
 
     def permute(j):
         for i2 in range(width // 256):
-            for s in range(2):
+            for s in range(3):
                 x = permuted(j, s, i2)
                 xs[j, s, 2 * i2] = x[:, :LANES]
                 xs[j, s, 2 * i2 + 1] = x[:, LANES:]
@@ -377,21 +372,21 @@
     def gather_plane(j):
         r1[j, me_q] = state[j, me_q]
         for n in range(plane - 1):
-            remote(state.at[j, q_rank[n]], r1.at[j, me_q], s1_send.at[j], s1_recv.at[j], q_peer[n]).start()
+            remote(state.at[j, q_rank[n]], r1.at[j, me_q], s1_send, s1_recv.at[j], q_peer[n]).start()
 
     def whole_1(j):
         others = pl.ds(0, plane - 1)
-        return remote(state.at[j, others], r1.at[j, others], s1_send.at[j], s1_recv.at[j], q_peer[0])
+        return remote(state.at[j, others], r1.at[j, others], s1_send, s1_recv.at[j], q_peer[0])
 
     def whole_3(j):
         others = pl.ds(0, plane - 1)
-        return remote(back.at[j, others], inflow.at[j, others], s3_send.at[j], s3_recv.at[j], q_peer[0])
+        return remote(back.at[j, others], inflow.at[j, others], s3_send, s3_recv.at[j], q_peer[0])
 
     def send_2(j, k):
-        return remote(total.at[j], r2.at[j, me_z], s2_send.at[j], s2_recv.at[j], z_later[k - 1])
-
-    def later_planes(j, distances):
-        for k in distances:
+        return remote(total.at[j], r2.at[j, me_z], s2_send, s2_recv.at[j], z_later[k - 1])
+
+    def later_planes(j):
+        for k in range(1, n_z):
 
             @pl.when(me_z + k < n_z)
             def _():
@@ -399,7 +394,7 @@
 
     def whole_2(j, count):
         those = pl.ds(0, count)
-        return remote(r2.at[j, those], r2.at[j, those], s2_send.at[j], s2_recv.at[j], z_later[0])
+        return remote(r2.at[j, those], r2.at[j, those], s2_send, s2_recv.at[j], z_later[0])
 
     def combine_plane(j):
         whole_1(j).wait_recv()
@@ -416,7 +411,7 @@
             run_i = ai + r1[j, e, 2:4, :]
         total[j, 0:2, :] = run_r
         total[j, 2:4, :] = run_i
-        later_planes(j, near_planes)
+        later_planes(j)
 
     def combine_all(j):
         for count in range(1, n_z):
@@ -444,15 +439,14 @@
             run_r, run_i = cmul(pr * keep, pi * keep, run_r, run_i)
         inflow[j, me_q] = back[j, me_q]
         for n in range(plane - 1):
-            remote(back.at[j, q_rank[n]], inflow.at[j, me_q], s3_send.at[j], s3_recv.at[j], q_peer[n]).start()
+            remote(back.at[j, q_rank[n]], inflow.at[j, me_q], s3_send, s3_recv.at[j], q_peer[n]).start()
 
     def response(j):
         @pl.loop(0, width // 256)
         def _(i2):
-            x2 = permuted(j, 2, i2)
             for h in range(2):
                 i = 2 * i2 + h
-                x = [x2[8 * k : 8 * k + 8, h * LANES : (h + 1) * LANES] for k in range(STEPS)]
+                x = steps_of(xs.at[j, 2, i])
                 gate = filters(j, i, par_b, 0, x)
                 head = first_two(j, 2, i, par_b, 0, x)
                 for k in range(2):
@@ -519,19 +513,14 @@
                     )
                 )
             mixed = jnp.concatenate(halves, axis=1).astype(BF16)
-            obuf[j, :, i2 * 256 : i2 * 256 + 256] = jnp.dot(perm_out[...], mixed, preferred_element_type=F32).astype(BF16)
+            lane = pl.ds(pl.multiple_of(block[j] * width + i2 * 256, 256), 256)
+            obuf[:, lane] = jnp.dot(perm_out[...], mixed, preferred_element_type=F32).astype(BF16)
         columns = pl.ds(pl.multiple_of(block[j] * width, width), width)
-        copy = pltpu.make_async_copy(obuf.at[j], out.at[0, :, columns], o_sem.at[j])
-        copy.start()
-        return copy
+        pltpu.make_async_copy(obuf.at[:, columns], out.at[0, :, columns], o_sem).start()
 
     for j in range(n_dp):
         permute(j)
     products(0)
-    if rounds:
-        learn(0)
-    if len(rounds) > 1:
-        tell(1)
     for j in range(1, n_dp):
         send_a(j).wait_recv()
         if j == n_dp - 1:
@@ -553,42 +542,39 @@
             gather_plane(0)
         states(j)
         gather_plane(j)
-    if len(rounds) > 1:
-        learn(1)
-    if len(rounds) > 2:
-        tell(2)
     response(0)
+    learn_later()
     for j in range(n_dp):
         combine_plane(j)
     for j in range(1, n_dp):
         send_b(j).wait_recv()
+        if j == n_dp - 1:
+            combine_all(0)
         response(j)
+    for j in range(1, n_dp):
+        combine_all(j)
     for j in range(n_dp):
-        combine_all(j)
-    if far_planes:
-        learn(2)
-    for j in range(n_dp):
-        later_planes(j, far_planes)
-    stores = [finish(j) for j in range(n_dp)]
+        finish(j)
 
     @pl.when(me + 1 < n_seq)
     def _():
         send_h().wait_send()
 
-    for j in range(n_dp):
-        if j:
-            send_a(j).wait_send()
-            send_b(j).wait_send()
-        whole_1(j).wait_send()
-        for count in range(1, n_z):
-
-            @pl.when(me_z + count == n_z - 1)
-            def _():
-                whole_2(j, count).wait_send()
-
-        whole_3(j).wait_send()
-    for copy in stores:
-        copy.wait()
+    for j in range(1, n_dp):
+        send_a(j).wait_send()
+    for j in range(1, n_dp):
+        send_b(j).wait_send()
+    others = pl.ds(0, plane - 1)
+    for source, target, sem in ((state, r1, s1_send), (back, inflow, s3_send)):
+        remote(source.at[:, others], target.at[:, others], sem, s1_recv.at[0], q_peer[0]).wait_send()
+    for count in range(1, n_z):
+
+        @pl.when(n_z - 1 - me_z == count)
+        def _():
+            those = r2.at[:, pl.ds(0, count)]
+            remote(those, those, s2_send, s2_recv.at[0], z_later[0]).wait_send()
+
+    pltpu.make_async_copy(obuf, out.at[0], o_sem).wait()
 
 
 def local(n_dp, n_seq, streams, short_filter, decay_rate, pole_angle, residue_re, residue_im, skip_gain, doc_starts):
@@ -610,9 +596,9 @@
             vmem((16, n_dp * width // 2), BF16),
             vmem((16, n_dp * width // 2), F32),
             vmem((n_dp * plane, 8, LANES), F32),
-            vmem((n_dp, 2, plane, TOK, LANES), F32),
+            vmem((n_dp, 3, plane, TOK, LANES), F32),
             vmem((n_dp, plane, 32, LANES), F32),
-            vmem((n_dp, TOK, width), BF16),
+            vmem((TOK, n_dp * width), BF16),
             vmem((3, 3, width), F32),
             vmem((2, width), F32),
             vmem((2, width), F32),
@@ -652,14 +638,14 @@
             dma((n_dp - 1,)),
             dma(()),
             dma(()),
+            dma(()),
             dma((n_dp,)),
+            dma(()),
             dma((n_dp,)),
+            dma(()),
             dma((n_dp,)),
-            dma((n_dp,)),
-            dma((n_dp,)),
-            dma((n_dp,)),
-            dma((n_dp,)),
-            pltpu.SemaphoreType.REGULAR((3,)),
+            dma(()),
+            pltpu.SemaphoreType.REGULAR,
         ],
         compiler_params=pltpu.CompilerParams(collective_id=0, has_side_effects=True, vmem_limit_bytes=48 * 2**20),
         name="hyena_modal_scan",

time: 24.3 us -> 22.3 us (0.918); the launches traced: 24.2 us -> 21.9 us
  Pallas kernels: 23.2 us -> 20.9 us
    pallas_call x1, Pallas kernels: 23.2 us -> 20.9 us  [local(): pl.pallas_call(functools.partial(kernel, n_dp, n_seq, plane), out_shape=j...]
where the time goes in v4:
time: 22.3 us; the launch traced here: 21.9 us
  Pallas kernels  20.9 us (94%)
  local copies, waits for them, and re-layouts  0.97 us (4%)
    pallas_call x1, Pallas kernels, local(): pl.pallas_call(functools.partial(kernel, n_dp, n_seq, plane), out_shape=j...  20.9 us
    unnamed x1, local copies, waits for them, and re-layouts  0.97 us

profile of v4, /device:TPU:225, one launch (start us, length us, event | category | flops | bytes accessed | tf_op | source)
XLA Modules:
  0.0 21.9 jit_solution(8173965818672540377)
XLA Ops:
  0.0 20.9 %hyena_modal_scan.1 = bf16[1,128,4096]{2,1,0:T(8,128)(2,1)S(1)} custom-call(bf16[3,1,128,4096]{3,2,1,0:T(8,128)(2,1)} %streams_hbm.1, f32[3,3,1024]{2,1,0:T(4,128)} %taps_hbm.1, f32[2,1024]{1,0:T(2,128)} %decay_hbm.1, f32[2,1024]{1,0:T(2,128)} %angle_hbm.1, f32[2,1024]{1,0:T(2,128)} %resr_hbm.1, f32[2,1024]{1,0:T(2,128)} %resi_hbm.1, f32[1,1024]{1,0:T(1,128)} %bitcast.1, ...), custom_call_target="tpu_custom_call" | custom-call | tf_op jit(solution)/shard_map/hyena_modal_scan/pallas_call | solution.py:588
  20.9 1.0 %copy.10 = bf16[1,128,4096]{2,1,0:T(8,128)(2,1)} copy(bf16[1,128,4096]{2,1,0:T(8,128)(2,1)S(1)} %hyena_modal_scan.1) | data formatting | bytes 2097152

commit v5 on v4

--- a/solution.py
+++ b/solution.py
@@ -548,11 +548,12 @@
         combine_plane(j)
     for j in range(1, n_dp):
         send_b(j).wait_recv()
-        if j == n_dp - 1:
-            combine_all(0)
-        response(j)
-    for j in range(1, n_dp):
+        if j < n_dp - 1 or n_dp == 2:
+            response(j)
+    for j in range(n_dp):
         combine_all(j)
+    if n_dp > 2:
+        response(n_dp - 1)
     for j in range(n_dp):
         finish(j)
 

time: 22.3 us -> 22 us (0.987); the launches traced: 21.9 us -> 21.9 us
  no operation moved by 1% of the time
where the time goes in v5:
time: 22 us; the launch traced here: 21.9 us
  Pallas kernels  20.9 us (95%)
  local copies, waits for them, and re-layouts  0.97 us (4%)
    pallas_call x1, Pallas kernels, local(): pl.pallas_call(functools.partial(kernel, n_dp, n_seq, plane), out_shape=j...  20.9 us
    unnamed x1, local copies, waits for them, and re-layouts  0.97 us

profile of v5, /device:TPU:225, one launch (start us, length us, event | category | flops | bytes accessed | tf_op | source)
XLA Modules:
  0.0 21.9 jit_solution(8725207953498292893)
XLA Ops:
  0.0 20.9 %hyena_modal_scan.1 = bf16[1,128,4096]{2,1,0:T(8,128)(2,1)S(1)} custom-call(bf16[3,1,128,4096]{3,2,1,0:T(8,128)(2,1)} %streams_hbm.1, f32[3,3,1024]{2,1,0:T(4,128)} %taps_hbm.1, f32[2,1024]{1,0:T(2,128)} %decay_hbm.1, f32[2,1024]{1,0:T(2,128)} %angle_hbm.1, f32[2,1024]{1,0:T(2,128)} %resr_hbm.1, f32[2,1024]{1,0:T(2,128)} %resi_hbm.1, f32[1,1024]{1,0:T(1,128)} %bitcast.1, ...), custom_call_target="tpu_custom_call" | custom-call | tf_op jit(solution)/shard_map/hyena_modal_scan/pallas_call | solution.py:589
  20.9 1.0 %copy.10 = bf16[1,128,4096]{2,1,0:T(8,128)(2,1)} copy(bf16[1,128,4096]{2,1,0:T(8,128)(2,1)S(1)} %hyena_modal_scan.1) | data formatting | bytes 2097152
